TPU v7x, 256 devices: a whole 4x4x8 slice. The times are simulated.
256 devices in a mesh: ray: 16 (over y, z_lo), pix: 16 (over z_hi, x, core).
Axes of the slice: x: 4, y: 4, z: 8 (z_hi: 2, z_lo: 4; z = z_hi * 4 + z_lo), core: 2. Of those that a mesh axis runs over, the one named last changes fastest.
Arguments:
- positions: float32 [2, 16384], P(None, 'ray'), may hold values from -2 to 2
- directions: float32 [2, 16384], P(None, 'ray'), may hold values from -0.35 to 0.35
- path: float32 [16384], P('ray'), may hold values from -9 to 9
- amplitude: float32 [16384], P('ray'), may hold values from 0.3 to 3
- psf_grad: float32 [3, 1024, 1024], P(None, 'pix', 'ray'), may hold values from -0.3 to 0.3
Outputs:
- psf: float32 [3, 1024, 1024], P(None, 'pix', 'ray')
- ray_grad: float32 [6, 16384], P(None, 'ray')
All inputs are finite; a program needn't handle non-finite values.
Results may differ from a plain program's by a relative error of at most 0.0054.
Values may be sent and summed in bfloat16 or wider, within the bound.
A program may use at most 192 MiB of HBM per device.

v0:
```python
import math

import jax
import jax.numpy as jnp
from jax import lax
from jax.sharding import PartitionSpec as P

NPIX = 1024


wave_scales = (1.2088, 1.0, 0.8953)
two_pi = 2.0 * math.pi


def centred(start, count):
    return (start + jnp.arange(count)).astype(jnp.float32) - 0.5 * NPIX + 0.5


def build_tables(rays, rows_x, cols_y, norm):
    row_list = []
    col_list = []
    weight = (rays[5] * norm)[:, None]
    for wave in range(3):
        scale = wave_scales[wave]
        angle = scale * (
            rays[4][:, None]
            + two_pi
            * (
                rays[2][:, None] * (rows_x[None, :] - rays[0][:, None])
                - rays[3][:, None] * rays[1][:, None]
            )
        )
        row_list.append(jnp.stack([weight * jnp.cos(angle), weight * jnp.sin(angle)]))
        beta = scale * two_pi * cols_y[:, None] * rays[3][None, :]
        col_list.append(jnp.stack([jnp.cos(beta), jnp.sin(beta)]))
    return (jnp.stack(row_list), jnp.stack(col_list))


def mixing(a_re, a_im):
    upper = jnp.concatenate([a_re, a_im], axis=1)
    lower = jnp.concatenate([-a_im, a_re], axis=1)
    return jnp.concatenate([upper, lower], axis=0).astype(jnp.bfloat16)


def product(left, right, dims):
    return lax.dot_general(left, right, dims, preferred_element_type=jnp.float32)


def block_count(count):
    return max(1, min(16, count // 256))


def field_terms(row_tab, col_tab):
    count = row_tab.shape[2]
    nblk = block_count(count)
    blk = count // nblk

    def step(index, total):
        a_blk = lax.dynamic_slice_in_dim(row_tab, index * blk, blk, 2)
        b_blk = lax.dynamic_slice_in_dim(col_tab, index * blk, blk, 3)
        parts = []
        for wave in range(3):
            left = jnp.concatenate([b_blk[wave, 0], b_blk[wave, 1]], axis=1).astype(jnp.bfloat16)
            parts.append(
                product(left, mixing(a_blk[wave, 0], a_blk[wave, 1]), (((1,), (0,)), ((), ())))
            )
        return total + jnp.concatenate(parts, axis=1)

    init = jnp.zeros((col_tab.shape[2], 6 * row_tab.shape[3]), jnp.float32)
    return lax.fori_loop(0, nblk, step, init)


def ray_partials(row_tab, col_tab, rows_x, cols_y, cotangent):
    count = row_tab.shape[2]
    nblk = block_count(count)
    blk = count // nblk
    plen = rows_x.shape[0]

    def one_block(index):
        a_blk = lax.dynamic_slice_in_dim(row_tab, index * blk, blk, 2)
        b_blk = lax.dynamic_slice_in_dim(col_tab, index * blk, blk, 3)
        first = jnp.zeros((blk,), jnp.float32)
        second = jnp.zeros((blk,), jnp.float32)
        third = jnp.zeros((blk,), jnp.float32)
        fourth = jnp.zeros((blk,), jnp.float32)
        for wave in range(3):
            scale = wave_scales[wave]
            a_re = a_blk[wave, 0]
            a_im = a_blk[wave, 1]
            b_re = b_blk[wave, 0]
            b_im = b_blk[wave, 1]
            left = jnp.concatenate([b_re, b_im], axis=1).astype(jnp.bfloat16)
            mix = mixing(a_re, a_im)
            grad_u = cotangent[:, 2 * plen * wave : 2 * plen * (wave + 1)]
            proj = product(left, grad_u, (((0,), (0,)), ((), ())))
            d_are = proj[:blk, :plen] + proj[blk:, plen:]
            d_aim = proj[:blk, plen:] - proj[blk:, :plen]
            d_b = product(grad_u, mix, (((1,), (1,)), ((), ())))
            d_beta = d_b[:, blk:] * b_re - d_b[:, :blk] * b_im
            d_alpha = d_aim * a_re - d_are * a_im
            first = first + scale * jnp.sum(d_alpha, axis=1)
            second = second + scale * two_pi * jnp.sum(d_alpha * rows_x[None, :], axis=1)
            third = third + scale * two_pi * jnp.sum(d_beta * cols_y[:, None], axis=0)
            fourth = fourth + jnp.sum(d_are * a_re + d_aim * a_im, axis=1)
        return jnp.stack([first, second, third, fourth])

    out = lax.map(one_block, jnp.arange(nblk))
    return jnp.transpose(out, (1, 0, 2)).reshape(4, count)


def finish(sums, rays):
    return jnp.stack(
        [
            sums[0],
            -two_pi * rays[2] * sums[0],
            -two_pi * rays[3] * sums[0],
            (sums[1] - two_pi * rays[0] * sums[0]) / NPIX,
            (sums[2] - two_pi * rays[1] * sums[0]) / NPIX,
            sums[3] / rays[5],
        ]
    )


def intensity(field, psf_grad, clen, plen):
    shaped = field.reshape(clen, 3, 2, plen)
    psf = jnp.transpose(shaped[:, :, 0] ** 2 + shaped[:, :, 1] ** 2, (1, 2, 0))
    weight = jnp.transpose(psf_grad, (2, 0, 1))
    grad_u = (2.0 * weight[:, :, None, :] * shaped).reshape(clen, 6 * plen).astype(jnp.bfloat16)
    return (psf, grad_u)


def on_device(positions, directions, path, amplitude, psf_grad):
    rays = jnp.concatenate([positions, directions, path[None], amplitude[None]], axis=0)
    local = rays.shape[1]
    plen = NPIX // lax.axis_size("pix")
    clen = NPIX // lax.axis_size("ray")
    norm = 1.0 / math.sqrt(local * lax.axis_size("ray"))
    rows_x = centred(lax.axis_index("pix") * plen, plen)
    all_cols = centred(0, NPIX)
    row_tab, col_tab = build_tables(rays, rows_x, all_cols, norm)
    field = lax.psum_scatter(field_terms(row_tab, col_tab), "ray", scatter_dimension=0, tiled=True)
    psf, grad_u = intensity(field, psf_grad, clen, plen)
    gathered = lax.all_gather(grad_u, "ray", axis=0, tiled=True)
    partial_value = ray_partials(row_tab, col_tab, rows_x, all_cols, gathered)
    sums = lax.psum(partial_value, "pix")
    return (psf, finish(sums, rays))


def solution(mesh):
    in_specs = (P(None, "ray"), P(None, "ray"), P("ray"), P("ray"), P(None, "pix", "ray"))
    out_specs = (P(None, "pix", "ray"), P(None, "ray"))
    return jax.shard_map(
        on_device, mesh=mesh, in_specs=in_specs, out_specs=out_specs, check_vma=False
    )
```

profile of v0, /device:TPU:1, one launch (start us, length us, event | category | flops | bytes accessed | tf_op | source)
XLA Modules:
  0.0 492.1 jit_solution(16539537502296417018)
XLA Ops:
  9.5 3.6 cosine_multiply_fusion.2
  13.2 46.6 %multiply_cosine_fusion.2 = (f32[1,1024,1024]{2,1,0:T(8,128)}, f32[1,1024,1024]{2,1,0:T(8,128)}, f32[1,1024,1024]{2,1,0:T(8,128)}, f32[1,1024,1024]{2,1,0:T(8,12...) fusion(f32[1024]{0:T(1024)S(1)} %bitcast.214, f32[1024]{0:T(1024)S(1)} %fusion.111, ...), kind=kLoop, calls=%fused_computation.186 | loop fusion | flops 3145728 | bytes 25182208 | tf_op jit(solution)/shard_map/cos | solution.py:35
  62.8 9.3 %maximum_bitcast_fusion.1 = (f32[1,2,1024,1024]{3,2,1,0:T(8,128)S(1)}, f32[1,2,1024,1024]{3,2,1,0:T(8,128)}) fusion(f32[1,1024,1024]{2,1,0:T(8,128)} %get-tuple-element.336, f32[1,1024,1024]{2,1,0:T(8,128)} %get-tuple-element.335, f32[1,1024,1024]{2,1,0:T(8,128)} %get-tuple-element.341, f32[1,1024,1024]{2,1,0:T(8,128)} %get-tuple-element.342), kind=kLoop, calls=%fused_computation.178 | loop fusion | flops 4194304 | bytes 33554432 | tf_op jit(solution)/shard_map/stack | solution.py:36
  72.1 15.7 %fusion.115 = (bf16[3,2,1024,1024]{3,2,1,0:T(8,128)(2,1)}, f32[3,2,1024,1024]{3,2,1,0:T(8,128)}) fusion(f32[1,2,1024,1024]{3,2,1,0:T(8,128)S(1)} %maximum_bitcast_fusion.3, f32[1,2,1024,1024]{3,2,1,0:T(8,128)} %get-tuple-element.346, f32[1,2,1024,1024]{3,2,1,0:T(8,128)S(1)} %get-tuple-element.345), kind=kLoop, calls=%fused_computation.219 | loop fusion | flops 18874368 | bytes 62914560
  87.8 56.3 %while.27 = (s32[]{:T(128)}, f32[1024,384]{0,1:T(8,128)S(1)}, bf16[3,2,1024,1024]{3,2,1,0:T(8,128)(2,1)}, f32[3,2,1024,64]{2,3,1,0:T(8,128)}, s32[]{:T(128)}, /*...) while((s32[]{:T(128)}, f32[1024,384]{0,1:T(8,128)S(1)}, bf16[3,2,1024,1024]{3,2,1,0:T(8,128)(2,1)}, ...), condition=%wide.region_1.0_spmd.clone, body=%wide.region_0.0_spmd.clone.sunk | while | flops 412237824 | bytes 23888080 | solution.py:70
  96.0 2.5 fusion.173
  110.1 2.5 fusion.173
  124.2 2.5 fusion.173
  138.2 2.5 fusion.173
  145.9 82.6 %reduce-scatter.4.cloned.1.call-done = f32[64,384]{1,0:T(8,128)} async-done(((f32[1024,384]{1,0:T(8,128)}), f32[64,384]{1,0:T(8,128)}) %reduce-scatter.4.cloned.1.call-update) | async-done | bytes 98320
  229.7 41.5 %all_gather.3 = bf16[1024,384]{1,0:T(8,128)(2,1)} all-gather(bf16[64,384]{1,0:T(8,128)(2,1)S(1)} %copy.31), channel_id=1, replica_groups=mesh['ray'=16,'pix'=16] {'ray'}, dimensions={0}, use_global_device_ids=true | all-gather | bytes 835584 | tf_op jit(solution)/shard_map/all_gather | solution.py:143
  271.2 118.7 %while.26 = (s32[]{:T(128)}, f32[4,4,256]{2,1,0:T(4,128)S(1)}, s32[4]{0:T(128)S(1)}, f32[3,2,1024,1024]{3,2,1,0:T(8,128)}, bf16[1024,384]{1,0:T(8,128)(2,1)}, /*...) while((s32[]{:T(128)}, f32[4,4,256]{2,1,0:T(4,128)S(1)}, ...), condition=%wide.region_16.17_spmd.clone.clone, body=%wide.region_3.16_spmd.clone.clone.sunk | while | flops 819468480 | bytes 79344528 | solution.py:107
  272.5 5.2 %constant_dynamic-slice_fusion.15 = (f32[1,1,1024,256]{3,2,1,0:T(8,128)S(1)}, f32[1,1,1024,256]{3,2,1,0:T(8,128)}, f32[1,1,1024,256]{3,2,1,0:T(8,128)}, f32[1,1,...) fusion(f32[3,2,1024,1024]{3,2,1,0:T(8,128)} %get-tuple-element.584, ...), kind=kLoop, calls=%fused_computation.102.clone.1 | loop fusion | bytes 12582924 | tf_op jit(solution)/shard_map/while/body/eval_jaxpr/slice | solution.py:90
  281.5 2.5 copy.70
  290.0 2.5 copy.68
  302.1 5.2 %constant_dynamic-slice_fusion.15 = (f32[1,1,1024,256]{3,2,1,0:T(8,128)S(1)}, f32[1,1,1024,256]{3,2,1,0:T(8,128)}, f32[1,1,1024,256]{3,2,1,0:T(8,128)}, f32[1,1,...) fusion(f32[3,2,1024,1024]{3,2,1,0:T(8,128)} %get-tuple-element.584, ...), kind=kLoop, calls=%fused_computation.102.clone.1 | loop fusion | bytes 12582924 | tf_op jit(solution)/shard_map/while/body/eval_jaxpr/slice | solution.py:90
  311.1 2.5 copy.70
  319.7 2.5 copy.68
  331.8 5.2 %constant_dynamic-slice_fusion.15 = (f32[1,1,1024,256]{3,2,1,0:T(8,128)S(1)}, f32[1,1,1024,256]{3,2,1,0:T(8,128)}, f32[1,1,1024,256]{3,2,1,0:T(8,128)}, f32[1,1,...) fusion(f32[3,2,1024,1024]{3,2,1,0:T(8,128)} %get-tuple-element.584, ...), kind=kLoop, calls=%fused_computation.102.clone.1 | loop fusion | bytes 12582924 | tf_op jit(solution)/shard_map/while/body/eval_jaxpr/slice | solution.py:90
  340.8 2.5 copy.70
  349.4 2.5 copy.68
  361.5 5.2 %constant_dynamic-slice_fusion.15 = (f32[1,1,1024,256]{3,2,1,0:T(8,128)S(1)}, f32[1,1,1024,256]{3,2,1,0:T(8,128)}, f32[1,1,1024,256]{3,2,1,0:T(8,128)}, f32[1,1,...) fusion(f32[3,2,1024,1024]{3,2,1,0:T(8,128)} %get-tuple-element.584, ...), kind=kLoop, calls=%fused_computation.102.clone.1 | loop fusion | bytes 12582924 | tf_op jit(solution)/shard_map/while/body/eval_jaxpr/slice | solution.py:90
  379.1 2.5 copy.68
  389.9 92.7 %psum.7 = f32[4,1024]{1,0:T(4,128)S(1)} all-reduce(f32[4,1024]{1,0:T(4,128)S(1)} %bitcast.219), channel_id=1, replica_groups=mesh['ray'=16,'pix'=16] {'pix'}, use_global_device_ids=true, to_apply=%region_17.18 | all-reduce | flops 4096 | bytes 32768 | tf_op jit(solution)/shard_map/psum | solution.py:145
  (249 shorter events, 133.7 us)
Async XLA Ops:
  7.2 221.3 %reduce-scatter.4.cloned.1.call-start = ((), (), s32[]{:S(2)}) async-start(), calls=%async_computation.1 | async-start | bytes 1671168
  144.2 1.8 copy-start.6
  229.5 41.7 %copy-start.5 = (f32[64,384]{0,1:T(8,128)}, f32[64,384]{0,1:T(8,128)S(1)}, u32[]{:S(2)}) copy-start(f32[64,384]{0,1:T(8,128)S(1)} %copy.38) | copy-start | bytes 294916
  271.2 211.4 %copy-start.7 = (f32[2,1024]{1,0:T(2,128)S(1)}, f32[2,1024]{1,0:T(2,128)}, u32[]{:S(2)}) copy-start(f32[2,1024]{1,0:T(2,128)} %param.10) | copy-start | bytes 24580
  271.2 211.4 %copy-start.8 = (f32[2,1024]{1,0:T(2,128)S(1)}, f32[2,1024]{1,0:T(2,128)}, u32[]{:S(2)}) copy-start(f32[2,1024]{1,0:T(2,128)} %param.9) | copy-start | bytes 24580
  271.2 211.4 %copy-start.9 = (f32[1024]{0:T(1024)S(1)}, f32[1024]{0:T(1024)}, u32[]{:S(2)}) copy-start(f32[1024]{0:T(1024)} %param.12) | copy-start | bytes 12292
  292.6 1.8 copy-start.3
  292.6 2.3 copy-start.4
  297.1 1.4 copy-start
  297.1 1.5 copy-start.1
  297.2 1.8 copy-start.2
  322.2 1.8 copy-start.3
  322.2 2.3 copy-start.4
  326.8 1.4 copy-start
  326.8 1.5 copy-start.1
  326.8 1.8 copy-start.2
  351.9 1.8 copy-start.3
  351.9 2.3 copy-start.4
  356.5 1.5 copy-start.1
  356.5 1.8 copy-start.2
  381.6 1.8 copy-start.3
  381.6 2.3 copy-start.4
  386.2 1.5 copy-start.1
  386.2 1.8 copy-start.2
  (2 other events, 2.8 us)
Sparse Core Ops, SparseCore 0:
  146.0 82.4 reduce-scatter.3
where the time goes:
time: 501 us; the launch traced here: 492 us
  blocking collectives  134 us (27%)
  other arithmetic  114 us (23%)
  local copies, waits for them, and re-layouts  98.7 us (20%)
  waiting for transfers between devices  82.6 us (16%)
  matrix products  44.4 us (9%)
  between operations  14.2 us (3%)
    psum x1, blocking collectives, on_device(): sums = lax.psum(partial_value, 'pix')  92.7 us
    unnamed x2, waiting for transfers between devices  82.6 us
    cos x1, other arithmetic, build_tables(): col_list.append(jnp.stack([jnp.cos(beta), jnp.sin(beta)]))  46.6 us
    dot_general x36, matrix products, product(): lax.dot_general(left, right, dims, preferred_element_type=jnp.float32)  44.4 us
    while x88, local copies, waits for them, and re-layouts  43.5 us
    all_gather x1, blocking collectives, on_device(): gathered = lax.all_gather(grad_u, 'ray', axis=0, tiled=True)  41.5 us
    slice x4, local copies, waits for them, and re-layouts, one_block(): b_re = b_blk[wave, 0]  20.6 us
    another operation x24, other arithmetic  16 us
  transfers between devices with their start and end apart: 1, of which 1 were waited for; matrix products, arithmetic and copies ran while one was open for 0% of the time, Pallas kernels for 0%

commit v1 on v0

v1 whole, which is shorter than its diff:
```python
import functools
import math

import jax
import jax.numpy as jnp
from jax import lax
from jax.experimental import pallas as pl
from jax.experimental.pallas import tpu as pltpu
from jax.sharding import PartitionSpec as P

NPIX = 1024

wave_scales = (1.2088, 1.0, 0.8953)
two_pi = 2.0 * math.pi
MESH = pl.DeviceIdType.MESH

COS_COEF = (
    0.9999999890590201,
    -19.739204499453688,
    64.93911745988827,
    -85.45013953077586,
    60.16763095018129,
    -25.96759924584206,
    6.528658157862129,
)
SIN_COEF = (
    6.283185302511498,
    -41.341700405316736,
    81.60513138576982,
    -76.70301535347629,
    42.02592698341473,
    -14.899846660399582,
    3.2381375010236435,
)


def horner(coef, z):
    total = coef[-1] * z + coef[-2]
    for c in coef[-3::-1]:
        total = total * z + c
    return total


def cos_sin_turns(turns):
    frac = turns - jnp.round(turns)
    z = frac * frac
    return horner(COS_COEF, z), horner(SIN_COEF, z) * frac


def ladder(base, step_c, step_s, ntiles, store):
    c0, s0 = base
    cc, ss, cs, sc = c0 * step_c, s0 * step_s, c0 * step_s, s0 * step_c
    twice = step_c + step_c
    up = (cc - ss, sc + cs)
    down = (cc + ss, sc - cs)
    mid = ntiles // 2
    store(mid, base, up)
    back, last = base, up
    for k in range(mid + 2, ntiles, 2):
        first = (twice * last[0] - back[0], twice * last[1] - back[1])
        second = (twice * first[0] - last[0], twice * first[1] - last[1])
        store(k, first, second)
        back, last = first, second
    back, last = base, down
    nxt = (twice * last[0] - back[0], twice * last[1] - back[1])
    store(mid - 2, nxt, last)
    back, last = last, nxt
    for k in range(mid - 4, -1, -2):
        second = (twice * last[0] - back[0], twice * last[1] - back[1])
        first = (twice * second[0] - last[0], twice * second[1] - last[1])
        store(k, first, second)
        back, last = second, first


def kernel(
    n_ray,
    n_pix,
    pos_ref,
    dir_ref,
    path_ref,
    amp_ref,
    grad_ref,
    psf_ref,
    out_ref,
    pay,
    xt,
    yt,
    yf,
    acc,
    g2,
    v_loc,
    v_rem,
    lhs,
    s_snd,
    s_rcv,
    tot,
    fin,
    pay_send,
    pay_recv,
    g_sem,
    v_sem,
    s_send,
    s_recv,
    t_send,
    t_recv,
    f_sem,
):
    me = lax.axis_index("ray")
    pix = lax.axis_index("pix")
    core = lax.rem(pix, 2)
    pair = lax.div(pix, 2)
    n_pair = n_pix // 2
    partner = pix + 1 - 2 * core
    rows = NPIX // n_pair
    cols = NPIX // n_ray
    half = pay.shape[2]
    count = 2 * half
    norm = 1.0 / math.sqrt(count * n_ray)

    def ray_peer(k):
        return {"ray": lax.rem(me + k, n_ray)}

    def pair_peer(k):
        return {"pix": lax.rem(pix + 2 * k, n_pix)}

    barrier = pltpu.get_barrier_semaphore()

    def greet_ray(k, carry):
        pl.semaphore_signal(barrier, inc=1, device_id=ray_peer(k), device_id_type=MESH)
        return carry

    def greet_pair(k, carry):
        pl.semaphore_signal(barrier, inc=1, device_id=pair_peer(k), device_id_type=MESH)
        return carry

    lax.fori_loop(1, n_ray, greet_ray, 0)
    lax.fori_loop(1, n_pair, greet_pair, 0)
    pl.semaphore_signal(barrier, inc=1, device_id={"pix": partner}, device_id_type=MESH)

    mine = pl.ds(pl.multiple_of(core * half, 128), half)
    l_own = dir_ref[0:1, mine]
    m_own = dir_ref[1:2, mine]
    pay[me, 0:1, :] = (
        path_ref[0:1, mine] * (1.0 / two_pi) - l_own * pos_ref[0:1, mine] - m_own * pos_ref[1:2, mine]
    )
    pay[me, 1:2, :] = l_own
    pay[me, 2:3, :] = m_own
    pay[me, 3:4, :] = amp_ref[0:1, mine] * norm
    for wave in range(3):
        g = grad_ref[wave]
        g2[core, wave] = jnp.concatenate([g, g], axis=1)

    pl.semaphore_wait(barrier, n_ray + n_pair - 1)

    def pay_copy(k, slot):
        return pltpu.make_async_remote_copy(
            src_ref=pay.at[me],
            dst_ref=pay.at[slot],
            send_sem=pay_send.at[k],
            recv_sem=pay_recv.at[slot],
            device_id=ray_peer(n_ray - k),
            device_id_type=MESH,
        )

    def send_pay(k, carry):
        pay_copy(k, me).start()
        return carry

    lax.fori_loop(1, n_ray, send_pay, 0)

    def g_copy(slot):
        return pltpu.make_async_remote_copy(
            src_ref=g2.at[core],
            dst_ref=g2.at[slot],
            send_sem=g_sem.at[0],
            recv_sem=g_sem.at[1],
            device_id={"pix": partner},
            device_id_type=MESH,
        )

    g_copy(core).start()

    row_start = pair * rows
    col_start = me * cols
    sub = lax.broadcasted_iota(jnp.int32, (8, half), 0)
    x_base = (sub + (row_start + rows // 2)).astype(jnp.float32) - (0.5 * NPIX - 0.5)
    y_base = (sub + (col_start + cols // 2)).astype(jnp.float32) - (0.5 * NPIX - 0.5)
    wave_of = lax.rem(sub, 3)
    step_scale = 8.0 * jnp.where(
        wave_of == 0, wave_scales[0], jnp.where(wave_of == 1, wave_scales[1], wave_scales[2])
    )

    acc[...] = jnp.zeros_like(acc)

    def forward(block):
        rho = jnp.broadcast_to(pay[block, 0:1, :], (8, half))
        l_all = jnp.broadcast_to(pay[block, 1:2, :], (8, half))
        m_all = jnp.broadcast_to(pay[block, 2:3, :], (8, half))
        amp = jnp.broadcast_to(pay[block, 3:4, :], (8, half))
        step_c, step_s = cos_sin_turns(step_scale * jnp.where(sub < 3, l_all, m_all))
        x_turns = rho + l_all * x_base
        y_turns = m_all * y_base
        for wave in range(3):
            scale = wave_scales[wave]

            def store_x(k, first, second):
                for part in range(2):
                    tile = jnp.concatenate([first[part], second[part]], axis=0)
                    at = part * rows + 8 * k
                    xt[wave, block, at : at + 16, :] = tile.astype(jnp.bfloat16)

            def store_y(k, first, second):
                for part in range(2):
                    tile = jnp.concatenate([first[part], second[part]], axis=0)
                    at = part * cols + 8 * k
                    yf[wave, block, at : at + 16, :] = tile
                    yt[wave, block, at : at + 16, :] = tile.astype(jnp.bfloat16)

            def row_of(table, index):
                return jnp.broadcast_to(table[index : index + 1, :], (8, half))

            bc, bs = cos_sin_turns(scale * x_turns)
            ladder((amp * bc, amp * bs), row_of(step_c, wave), row_of(step_s, wave), rows // 8, store_x)
            ladder(
                cos_sin_turns(scale * y_turns),
                row_of(step_c, wave + 3),
                row_of(step_s, wave + 3),
                cols // 8,
                store_y,
            )
            acc[wave] += lax.dot_general(
                xt[wave, block],
                yt[wave, block],
                (((1,), (1,)), ((), ())),
                preferred_element_type=jnp.float32,
            )

    forward(me)

    def forward_step(k, carry):
        block = lax.rem(me + k, n_ray)
        pay_copy(k, block).wait_recv()
        forward(block)
        return carry

    lax.fori_loop(1, n_ray, forward_step, 0)

    low = lax.broadcasted_iota(jnp.int32, (rows, 2 * cols), 1) < cols
    for wave in range(3):
        other = acc[wave, rows : 2 * rows, :]
        v_loc[wave] = acc[wave, 0:rows, :] + pltpu.roll(jnp.where(low, other, -other), cols, 1)

    v_copy = pltpu.make_async_remote_copy(
        src_ref=v_loc,
        dst_ref=v_rem,
        send_sem=v_sem.at[0],
        recv_sem=v_sem.at[1],
        device_id={"pix": partner},
        device_id_type=MESH,
    )
    v_copy.start()
    g_copy(1 - core).wait_recv()
    v_copy.wait_recv()

    own_rows = pl.ds(pl.multiple_of(core * (rows // 2), 8), rows // 2)
    offset = (lax.broadcasted_iota(jnp.int32, (2 * cols // 2, rows), 1)).astype(jnp.float32) - (
        0.5 * rows - 0.5
    )
    for wave in range(3):
        own = v_loc[wave, own_rows, :] + v_rem[wave, own_rows, :]
        power = own * own
        psf_ref[wave] = (power + pltpu.roll(power, cols, 1))[:, :cols]
        field = v_loc[wave] + v_rem[wave]
        weight = jnp.concatenate([g2[0, wave], g2[1, wave]], axis=0)
        grad_t = jnp.transpose(2.0 * weight * field)
        re = grad_t[:cols]
        im = grad_t[cols:]
        lhs[wave, 0:cols, 0:rows] = re.astype(jnp.bfloat16)
        lhs[wave, 0:cols, rows:] = im.astype(jnp.bfloat16)
        lhs[wave, cols : 2 * cols, 0:rows] = im.astype(jnp.bfloat16)
        lhs[wave, cols : 2 * cols, rows:] = (-re).astype(jnp.bfloat16)
        re = re * offset
        im = im * offset
        lhs[wave, 2 * cols : 3 * cols, 0:rows] = re.astype(jnp.bfloat16)
        lhs[wave, 2 * cols : 3 * cols, rows:] = im.astype(jnp.bfloat16)
        lhs[wave, 3 * cols :, 0:rows] = im.astype(jnp.bfloat16)
        lhs[wave, 3 * cols :, rows:] = (-re).astype(jnp.bfloat16)

    x_mid = (row_start + rows // 2).astype(jnp.float32) - 0.5 * NPIX
    y_mid = (col_start + cols // 2).astype(jnp.float32) - 0.5 * NPIX

    def s_copy(block, slot):
        return pltpu.make_async_remote_copy(
            src_ref=s_snd.at[block],
            dst_ref=s_rcv.at[slot],
            send_sem=s_send.at[block],
            recv_sem=s_recv.at[slot],
            device_id={"ray": block},
            device_id_type=MESH,
        )

    def backward(block):
        s1 = jnp.zeros((8, half), jnp.float32)
        s2 = jnp.zeros((8, half), jnp.float32)
        s3 = jnp.zeros((8, half), jnp.float32)
        s4 = jnp.zeros((8, half), jnp.float32)
        sub_f = sub.astype(jnp.float32)
        for wave in range(3):
            d_b = lax.dot_general(
                lhs[wave],
                xt[wave, block],
                (((1,), (0,)), ((), ())),
                preferred_element_type=jnp.float32,
            )
            zi = jnp.zeros((8, half), jnp.float32)
            zx = jnp.zeros((8, half), jnp.float32)
            zy = jnp.zeros((8, half), jnp.float32)
            for t in range(cols // 8):
                at = 8 * t
                br = yf[wave, block, at : at + 8, :]
                bi = yf[wave, block, cols + at : cols + at + 8, :]
                dbr = d_b[at : at + 8]
                dbi = d_b[cols + at : cols + at + 8]
                dxr = d_b[2 * cols + at : 2 * cols + at + 8]
                dxi = d_b[3 * cols + at : 3 * cols + at + 8]
                d = br * dbi - bi * dbr
                zi = zi + d
                zy = zy + d * (sub_f + (at - 0.5 * cols + 0.5))
                zx = zx + (br * dxi - bi * dxr)
                s4 = s4 + (br * dbr + bi * dbi)
            scale = wave_scales[wave]
            s1 = s1 + scale * zi
            s2 = s2 + (scale * two_pi) * (x_mid * zi + zx)
            s3 = s3 + (scale * two_pi) * (y_mid * zi + zy)
        return [jnp.sum(s, axis=0, keepdims=True) for s in (s1, s2, s3, s4)]

    def backward_step(k, carry):
        block = lax.rem(me + k, n_ray)
        for i, s in enumerate(backward(block)):
            s_snd[block, i : i + 1, :] = s
        s_copy(block, me).start()
        return carry

    lax.fori_loop(1, n_ray, backward_step, 0)
    for i, s in enumerate(backward(me)):
        s_rcv[me, i : i + 1, :] = s

    def wait_s(k, carry):
        block = lax.rem(me + k, n_ray)
        s_copy(block, block).wait_recv()
        return carry

    lax.fori_loop(1, n_ray, wait_s, 0)
    total = s_rcv[0]
    for b in range(1, n_ray):
        total = total + s_rcv[b]
    tot[pair] = total

    def t_copy(k, slot):
        return pltpu.make_async_remote_copy(
            src_ref=tot.at[pair],
            dst_ref=tot.at[slot],
            send_sem=t_send.at[k],
            recv_sem=t_recv.at[slot],
            device_id=pair_peer(k),
            device_id_type=MESH,
        )

    def send_t(k, carry):
        t_copy(k, pair).start()
        return carry

    def wait_t(k, carry):
        t_copy(k, lax.rem(pair + k, n_pair)).wait_recv()
        return carry

    lax.fori_loop(1, n_pair, send_t, 0)
    lax.fori_loop(1, n_pair, wait_t, 0)
    total = tot[0]
    for b in range(1, n_pair):
        total = total + tot[b]
    fin[core] = total

    def f_copy(slot):
        return pltpu.make_async_remote_copy(
            src_ref=fin.at[core],
            dst_ref=fin.at[slot],
            send_sem=f_sem.at[0],
            recv_sem=f_sem.at[1],
            device_id={"pix": partner},
            device_id_type=MESH,
        )

    f_copy(core).start()
    f_copy(1 - core).wait_recv()

    for h in range(2):
        at = slice(h * half, (h + 1) * half)
        s1 = fin[h, 0:1, :]
        out_ref[0:1, at] = s1
        out_ref[1:2, at] = -two_pi * dir_ref[0:1, at] * s1
        out_ref[2:3, at] = -two_pi * dir_ref[1:2, at] * s1
        out_ref[3:4, at] = (fin[h, 1:2, :] - two_pi * pos_ref[0:1, at] * s1) * (1.0 / NPIX)
        out_ref[4:5, at] = (fin[h, 2:3, :] - two_pi * pos_ref[1:2, at] * s1) * (1.0 / NPIX)
        out_ref[5:6, at] = fin[h, 3:4, :] / amp_ref[0:1, at]

    def drain_ray(k, carry):
        pay_copy(k, me).wait_send()
        s_copy(lax.rem(me + k, n_ray), me).wait_send()
        return carry

    def drain_pair(k, carry):
        t_copy(k, pair).wait_send()
        return carry

    lax.fori_loop(1, n_ray, drain_ray, 0)
    lax.fori_loop(1, n_pair, drain_pair, 0)
    g_copy(core).wait_send()
    v_copy.wait_send()
    f_copy(core).wait_send()


def on_device(n_ray, n_pix, positions, directions, path, amplitude, psf_grad):
    count = positions.shape[1]
    half = count // 2
    n_pair = n_pix // 2
    rows = NPIX // n_pair
    cols = NPIX // n_ray
    f32 = jnp.float32
    bf16 = jnp.bfloat16
    vmem = pl.BlockSpec(memory_space=pltpu.VMEM)
    dma = pltpu.SemaphoreType.DMA
    return pl.pallas_call(
        functools.partial(kernel, n_ray, n_pix),
        out_shape=(
            jax.ShapeDtypeStruct(psf_grad.shape, f32),
            jax.ShapeDtypeStruct((6, count), f32),
        ),
        in_specs=[vmem] * 5,
        out_specs=(vmem, vmem),
        scratch_shapes=[
            pltpu.VMEM((n_ray, 4, half), f32),
            pltpu.VMEM((3, n_ray, 2 * rows, half), bf16),
            pltpu.VMEM((3, n_ray, 2 * cols, half), bf16),
            pltpu.VMEM((3, n_ray, 2 * cols, half), f32),
            pltpu.VMEM((3, 2 * rows, 2 * cols), f32),
            pltpu.VMEM((2, 3, rows // 2, 2 * cols), f32),
            pltpu.VMEM((3, rows, 2 * cols), f32),
            pltpu.VMEM((3, rows, 2 * cols), f32),
            pltpu.VMEM((3, 4 * cols, 2 * rows), bf16),
            pltpu.VMEM((n_ray, 4, half), f32),
            pltpu.VMEM((n_ray, 4, half), f32),
            pltpu.VMEM((n_pair, 4, half), f32),
            pltpu.VMEM((2, 4, half), f32),
            dma((n_ray,)),
            dma((n_ray,)),
            dma((2,)),
            dma((2,)),
            dma((n_ray,)),
            dma((n_ray,)),
            dma((n_pair,)),
            dma((n_pair,)),
            dma((2,)),
        ],
        compiler_params=pltpu.CompilerParams(
            collective_id=0, has_side_effects=True, vmem_limit_bytes=56 * 1024 * 1024
        ),
        name="ray_wave",
    )(positions, directions, path.reshape(1, count), amplitude.reshape(1, count), psf_grad)


def solution(mesh):
    in_specs = (P(None, "ray"), P(None, "ray"), P("ray"), P("ray"), P(None, "pix", "ray"))
    out_specs = (P(None, "pix", "ray"), P(None, "ray"))
    body = functools.partial(on_device, mesh.shape["ray"], mesh.shape["pix"])
    return jax.shard_map(
        body, mesh=mesh, in_specs=in_specs, out_specs=out_specs, check_vma=False
    )
```

time: 501 us -> 45.8 us (0.09); the launches traced: 492 us -> 45.7 us
  blocking collectives: 134 us -> 0 us
  other arithmetic: 114 us -> 0 us
  local copies, waits for them, and re-layouts: 98.7 us -> 2.16 us
  waiting for transfers between devices: 82.6 us -> 0 us
  matrix products: 44.4 us -> 0 us
  Pallas kernels: 0 us -> 42.9 us
  between operations: 14.2 us -> 0.65 us
    psum x1 -> x0, blocking collectives: 92.7 us -> none  [on_device(): sums = lax.psum(partial_value, 'pix')]
    unnamed x2 -> x0, waiting for transfers between devices: 82.6 us -> none
    cos x1 -> x0, other arithmetic: 46.6 us -> none  [build_tables(): col_list.append(jnp.stack([jnp.cos(beta), jnp.sin(beta)]))]
    dot_general x36 -> x0, matrix products: 44.4 us -> none  [product(): lax.dot_general(left, right, dims, preferred_element_type=jnp.float32)]
    while x88 -> x0, local copies, waits for them, and re-layouts: 43.5 us -> none
    pallas_call x0 -> x1, Pallas kernels: none -> 42.9 us  [on_device(): pl.pallas_call(functools.partial(kernel, n_ray, n_pix), out_shape=(jax.Sh...]
    all_gather x1 -> x0, blocking collectives: 41.5 us -> none  [on_device(): gathered = lax.all_gather(grad_u, 'ray', axis=0, tiled=True)]
    slice x15 -> x0, local copies, waits for them, and re-layouts: 30.5 us -> none  [the longest x4 20.6 us: one_block(): b_re = b_blk[wave, 0]]
  transfers between devices with their start and end apart: 1 -> 0, of which waited for: 1 -> 0; matrix products, arithmetic and copies ran while one was open for 0% -> 0% of each run, Pallas kernels for 0% -> 0%
where the time goes in v1:
time: 45.8 us; the launch traced here: 45.7 us
  Pallas kernels  42.9 us (94%)
  local copies, waits for them, and re-layouts  2.16 us (5%)
  between operations  0.65 us (1%)
    pallas_call x1, Pallas kernels, on_device(): pl.pallas_call(functools.partial(kernel, n_ray, n_pix), out_shape=(jax.Sh...  42.9 us
    unnamed x4, local copies, waits for them, and re-layouts  2.16 us

profile of v1, /device:TPU:1, one launch (start us, length us, event | category | flops | bytes accessed | tf_op | source)
XLA Modules:
  0.0 45.7 jit_solution(11178476401144943259)
XLA Ops:
  0.6 42.9 %ray_wave.1 = (f32[3,64,64]{2,1,0:T(8,128)}, f32[6,1024]{1,0:T(8,128)}) custom-call(f32[2,1024]{1,0:T(2,128)} %pos_ref.1, f32[2,1024]{1,0:T(2,128)} %dir_ref.1, f32[1,1024]{1,0:T(1,128)} %bitcast.2, f32[1,1024]{1,0:T(1,128)} %bitcast.3, f32[3,64,64]{2,1,0:T(8,128)} %grad_ref.1), custom_call_target="tpu_custom_call" | custom-call | tf_op jit(solution)/shard_map/ray_wave/pallas_call | solution.py:433
  43.5 0.0 copy-start
  43.5 1.5 %copy.9 = f32[3,64,64]{2,1,0:T(8,128)} copy(f32[3,64,64]{2,1,0:T(8,128)} %get-tuple-element.4) | data formatting | bytes 98304
  45.1 0.0 copy-done
  45.1 0.6 %copy.10 = f32[6,1024]{1,0:T(8,128)} copy(f32[6,1024]{1,0:T(8,128)S(1)} %copy-done) | data formatting | bytes 49152
Async XLA Ops:
  43.5 1.6 %copy-start = (f32[6,1024]{1,0:T(8,128)S(1)}, f32[6,1024]{1,0:T(8,128)}, u32[]{:S(2)}) copy-start(f32[6,1024]{1,0:T(8,128)} %get-tuple-element.5) | copy-start | bytes 73732

commit v2 on v1

--- a/solution.py
+++ b/solution.py
@@ -72,9 +72,24 @@
         back, last = second, first
 
 
+def offset_of(k):
+    b, a = k >> 2, k & 3
+    b3, a3 = (b >> 1) * (b & 1), (a >> 1) * (a & 1)
+    dy = b + (b >> 1) - 2 * b3
+    dz = a + 5 * (a >> 1) - 6 * a3 + 4 * a3 * (dy & 1)
+    return dy, dz
+
+
 def kernel(
     n_ray,
     n_pix,
+    pos_hbm,
+    dir_hbm,
+    path_hbm,
+    amp_hbm,
+    grad_hbm,
+    psf_hbm,
+    out_hbm,
     pos_ref,
     dir_ref,
     path_ref,
@@ -94,7 +109,8 @@
     s_snd,
     s_rcv,
     tot,
-    fin,
+    in_sem,
+    out_sem,
     pay_send,
     pay_recv,
     g_sem,
@@ -103,12 +119,14 @@
     s_recv,
     t_send,
     t_recv,
-    f_sem,
 ):
     me = lax.axis_index("ray")
     pix = lax.axis_index("pix")
-    core = lax.rem(pix, 2)
-    pair = lax.div(pix, 2)
+    core = pix & 1
+    pair = pix >> 1
+    x_pos = pair & 3
+    y_pos = me >> 2
+    z_pos = 4 * (pair >> 2) + (me & 3)
     n_pair = n_pix // 2
     partner = pix + 1 - 2 * core
     rows = NPIX // n_pair
@@ -117,26 +135,47 @@
     count = 2 * half
     norm = 1.0 / math.sqrt(count * n_ray)
 
-    def ray_peer(k):
-        return {"ray": lax.rem(me + k, n_ray)}
-
-    def pair_peer(k):
-        return {"pix": lax.rem(pix + 2 * k, n_pix)}
+    def chip_at(dy, dz):
+        y = (y_pos + dy) & 3
+        z = (z_pos + dz) & 7
+        return {"ray": 4 * y + (z & 3), "pix": 8 * (z >> 2) + (pix & 7)}
+
+    def block_of(k):
+        dy, dz = offset_of(k)
+        return 4 * ((y_pos + dy) & 3) + ((z_pos + dz) & 3)
+
+    loads = [
+        pltpu.make_async_copy(src, dst, in_sem.at[i])
+        for i, (src, dst) in enumerate(
+            (
+                (pos_hbm, pos_ref),
+                (dir_hbm, dir_ref),
+                (path_hbm, path_ref),
+                (amp_hbm, amp_ref),
+                (grad_hbm, grad_ref),
+            )
+        )
+    ]
+    for load in loads:
+        load.start()
+
+    def wait_bytes(ref, sem):
+        pltpu.make_async_copy(ref, ref, sem).wait()
 
     barrier = pltpu.get_barrier_semaphore()
 
-    def greet_ray(k, carry):
-        pl.semaphore_signal(barrier, inc=1, device_id=ray_peer(k), device_id_type=MESH)
-        return carry
-
-    def greet_pair(k, carry):
-        pl.semaphore_signal(barrier, inc=1, device_id=pair_peer(k), device_id_type=MESH)
-        return carry
-
-    lax.fori_loop(1, n_ray, greet_ray, 0)
-    lax.fori_loop(1, n_pair, greet_pair, 0)
-    pl.semaphore_signal(barrier, inc=1, device_id={"pix": partner}, device_id_type=MESH)
-
+    def x_peer(dx, other):
+        return {"pix": (pix & 8) + 2 * ((x_pos + dx) & 3) + (core + other - 2 * core * other)}
+
+    x_others = [(dx, other) for dx in range(4) for other in range(2)][1:]
+
+    for dy, dz in [(dy, dz) for dy in range(4) for dz in (0, 1, 7, 2, 6)][1:]:
+        pl.semaphore_signal(barrier, inc=1, device_id=chip_at(dy, dz), device_id_type=MESH)
+    for dx, other in x_others:
+        pl.semaphore_signal(barrier, inc=1, device_id=x_peer(dx, other), device_id_type=MESH)
+
+    for load in loads[:4]:
+        load.wait()
     mine = pl.ds(pl.multiple_of(core * half, 128), half)
     l_own = dir_ref[0:1, mine]
     m_own = dir_ref[1:2, mine]
@@ -146,27 +185,27 @@
     pay[me, 1:2, :] = l_own
     pay[me, 2:3, :] = m_own
     pay[me, 3:4, :] = amp_ref[0:1, mine] * norm
+
+    pl.semaphore_wait(barrier, 26)
+
+    def pay_copy(k, slot):
+        dy, dz = offset_of(k)
+        return pltpu.make_async_remote_copy(
+            src_ref=pay.at[me],
+            dst_ref=pay.at[slot],
+            send_sem=pay_send.at[0],
+            recv_sem=pay_recv.at[slot],
+            device_id=chip_at(4 - dy, 8 - dz),
+            device_id_type=MESH,
+        )
+
+    for k in range(1, n_ray):
+        pay_copy(k, me).start()
+
+    loads[4].wait()
     for wave in range(3):
         g = grad_ref[wave]
         g2[core, wave] = jnp.concatenate([g, g], axis=1)
-
-    pl.semaphore_wait(barrier, n_ray + n_pair - 1)
-
-    def pay_copy(k, slot):
-        return pltpu.make_async_remote_copy(
-            src_ref=pay.at[me],
-            dst_ref=pay.at[slot],
-            send_sem=pay_send.at[k],
-            recv_sem=pay_recv.at[slot],
-            device_id=ray_peer(n_ray - k),
-            device_id_type=MESH,
-        )
-
-    def send_pay(k, carry):
-        pay_copy(k, me).start()
-        return carry
-
-    lax.fori_loop(1, n_ray, send_pay, 0)
 
     def g_copy(slot):
         return pltpu.make_async_remote_copy(
@@ -238,7 +277,7 @@
     forward(me)
 
     def forward_step(k, carry):
-        block = lax.rem(me + k, n_ray)
+        block = block_of(k)
         pay_copy(k, block).wait_recv()
         forward(block)
         return carry
@@ -286,16 +325,22 @@
         lhs[wave, 3 * cols :, 0:rows] = im.astype(jnp.bfloat16)
         lhs[wave, 3 * cols :, rows:] = (-re).astype(jnp.bfloat16)
 
+    psf_store = pltpu.make_async_copy(psf_ref, psf_hbm, out_sem.at[0])
+    psf_store.start()
+
     x_mid = (row_start + rows // 2).astype(jnp.float32) - 0.5 * NPIX
     y_mid = (col_start + cols // 2).astype(jnp.float32) - 0.5 * NPIX
 
-    def s_copy(block, slot):
+    here = 8 * y_pos + z_pos
+
+    def s_copy(k, far):
+        dy, dz = offset_of(k)
         return pltpu.make_async_remote_copy(
-            src_ref=s_snd.at[block],
-            dst_ref=s_rcv.at[slot],
-            send_sem=s_send.at[block],
-            recv_sem=s_recv.at[slot],
-            device_id={"ray": block},
+            src_ref=s_snd.at[k],
+            dst_ref=s_rcv.at[here],
+            send_sem=s_send.at[0],
+            recv_sem=s_recv.at[0],
+            device_id=chip_at(dy, dz + 4 * far),
             device_id_type=MESH,
         )
 
@@ -332,92 +377,63 @@
             s1 = s1 + scale * zi
             s2 = s2 + (scale * two_pi) * (x_mid * zi + zx)
             s3 = s3 + (scale * two_pi) * (y_mid * zi + zy)
-        return [jnp.sum(s, axis=0, keepdims=True) for s in (s1, s2, s3, s4)]
-
-    def backward_step(k, carry):
-        block = lax.rem(me + k, n_ray)
-        for i, s in enumerate(backward(block)):
-            s_snd[block, i : i + 1, :] = s
-        s_copy(block, me).start()
+        sums = [jnp.sum(s, axis=0, keepdims=True) for s in (s1, s2, s3, s4)]
+        return jnp.concatenate(
+            [s[:, 128 * t : 128 * t + 128] for s in sums for t in range(half // 128)], axis=0
+        )
+
+    def backward_step(i, carry):
+        k = n_ray - i
+        s_snd[k] = backward(block_of(k)).astype(jnp.bfloat16)
+        s_copy(k, 1).start()
+        s_copy(k, 0).start()
         return carry
 
     lax.fori_loop(1, n_ray, backward_step, 0)
-    for i, s in enumerate(backward(me)):
-        s_rcv[me, i : i + 1, :] = s
-
-    def wait_s(k, carry):
-        block = lax.rem(me + k, n_ray)
-        s_copy(block, block).wait_recv()
-        return carry
-
-    lax.fori_loop(1, n_ray, wait_s, 0)
-    total = s_rcv[0]
-    for b in range(1, n_ray):
-        total = total + s_rcv[b]
-    tot[pair] = total
-
-    def t_copy(k, slot):
-        return pltpu.make_async_remote_copy(
-            src_ref=tot.at[pair],
-            dst_ref=tot.at[slot],
-            send_sem=t_send.at[k],
-            recv_sem=t_recv.at[slot],
-            device_id=pair_peer(k),
+    s_own = backward(me).astype(jnp.bfloat16)
+    s_snd[0] = s_own
+    s_copy(0, 1).start()
+    s_rcv[here] = s_own
+    wait_bytes(s_rcv.at[0:31], s_recv.at[0])
+    total = s_rcv[0].astype(jnp.float32)
+    for b in range(1, 32):
+        total = total + s_rcv[b].astype(jnp.float32)
+    tot[4 * core + x_pos] = total
+
+    for dx, other in x_others:
+        pltpu.make_async_remote_copy(
+            src_ref=tot.at[4 * core + x_pos],
+            dst_ref=tot.at[4 * core + x_pos],
+            send_sem=t_send.at[0],
+            recv_sem=t_recv.at[0],
+            device_id=x_peer(dx, other),
             device_id_type=MESH,
-        )
-
-    def send_t(k, carry):
-        t_copy(k, pair).start()
-        return carry
-
-    def wait_t(k, carry):
-        t_copy(k, lax.rem(pair + k, n_pair)).wait_recv()
-        return carry
-
-    lax.fori_loop(1, n_pair, send_t, 0)
-    lax.fori_loop(1, n_pair, wait_t, 0)
-    total = tot[0]
-    for b in range(1, n_pair):
-        total = total + tot[b]
-    fin[core] = total
-
-    def f_copy(slot):
-        return pltpu.make_async_remote_copy(
-            src_ref=fin.at[core],
-            dst_ref=fin.at[slot],
-            send_sem=f_sem.at[0],
-            recv_sem=f_sem.at[1],
-            device_id={"pix": partner},
-            device_id_type=MESH,
-        )
-
-    f_copy(core).start()
-    f_copy(1 - core).wait_recv()
-
+        ).start()
+    wait_bytes(tot.at[0:7], t_recv.at[0])
+    tiles = half // 128
     for h in range(2):
-        at = slice(h * half, (h + 1) * half)
-        s1 = fin[h, 0:1, :]
-        out_ref[0:1, at] = s1
-        out_ref[1:2, at] = -two_pi * dir_ref[0:1, at] * s1
-        out_ref[2:3, at] = -two_pi * dir_ref[1:2, at] * s1
-        out_ref[3:4, at] = (fin[h, 1:2, :] - two_pi * pos_ref[0:1, at] * s1) * (1.0 / NPIX)
-        out_ref[4:5, at] = (fin[h, 2:3, :] - two_pi * pos_ref[1:2, at] * s1) * (1.0 / NPIX)
-        out_ref[5:6, at] = fin[h, 3:4, :] / amp_ref[0:1, at]
-
-    def drain_ray(k, carry):
-        pay_copy(k, me).wait_send()
-        s_copy(lax.rem(me + k, n_ray), me).wait_send()
-        return carry
-
-    def drain_pair(k, carry):
-        t_copy(k, pair).wait_send()
-        return carry
-
-    lax.fori_loop(1, n_ray, drain_ray, 0)
-    lax.fori_loop(1, n_pair, drain_pair, 0)
+        total = tot[4 * h]
+        for b in range(1, 4):
+            total = total + tot[4 * h + b]
+        for t in range(tiles):
+            at = slice(h * half + 128 * t, h * half + 128 * t + 128)
+            s1, s2, s3, s4 = (total[tiles * i + t : tiles * i + t + 1] for i in range(4))
+            out_ref[0:1, at] = s1
+            out_ref[1:2, at] = -two_pi * dir_ref[0:1, at] * s1
+            out_ref[2:3, at] = -two_pi * dir_ref[1:2, at] * s1
+            out_ref[3:4, at] = (s2 - two_pi * pos_ref[0:1, at] * s1) * (1.0 / NPIX)
+            out_ref[4:5, at] = (s3 - two_pi * pos_ref[1:2, at] * s1) * (1.0 / NPIX)
+            out_ref[5:6, at] = s4 / amp_ref[0:1, at]
+    out_store = pltpu.make_async_copy(out_ref, out_hbm, out_sem.at[1])
+    out_store.start()
+
+    wait_bytes(pay.at[0 : n_ray - 1], pay_send.at[0])
+    wait_bytes(s_rcv.at[0:31], s_send.at[0])
+    wait_bytes(tot.at[0:7], t_send.at[0])
     g_copy(core).wait_send()
     v_copy.wait_send()
-    f_copy(core).wait_send()
+    psf_store.wait()
+    out_store.wait()
 
 
 def on_device(n_ray, n_pix, positions, directions, path, amplitude, psf_grad):
@@ -428,7 +444,7 @@
     cols = NPIX // n_ray
     f32 = jnp.float32
     bf16 = jnp.bfloat16
-    vmem = pl.BlockSpec(memory_space=pltpu.VMEM)
+    any_space = pl.BlockSpec(memory_space=pl.ANY)
     dma = pltpu.SemaphoreType.DMA
     return pl.pallas_call(
         functools.partial(kernel, n_ray, n_pix),
@@ -436,9 +452,16 @@
             jax.ShapeDtypeStruct(psf_grad.shape, f32),
             jax.ShapeDtypeStruct((6, count), f32),
         ),
-        in_specs=[vmem] * 5,
-        out_specs=(vmem, vmem),
+        in_specs=[any_space] * 5,
+        out_specs=(any_space, any_space),
         scratch_shapes=[
+            pltpu.VMEM((2, count), f32),
+            pltpu.VMEM((2, count), f32),
+            pltpu.VMEM((1, count), f32),
+            pltpu.VMEM((1, count), f32),
+            pltpu.VMEM(psf_grad.shape, f32),
+            pltpu.VMEM(psf_grad.shape, f32),
+            pltpu.VMEM((6, count), f32),
             pltpu.VMEM((n_ray, 4, half), f32),
             pltpu.VMEM((3, n_ray, 2 * rows, half), bf16),
             pltpu.VMEM((3, n_ray, 2 * cols, half), bf16),
@@ -448,19 +471,19 @@
             pltpu.VMEM((3, rows, 2 * cols), f32),
             pltpu.VMEM((3, rows, 2 * cols), f32),
             pltpu.VMEM((3, 4 * cols, 2 * rows), bf16),
-            pltpu.VMEM((n_ray, 4, half), f32),
-            pltpu.VMEM((n_ray, 4, half), f32),
-            pltpu.VMEM((n_pair, 4, half), f32),
-            pltpu.VMEM((2, 4, half), f32),
-            dma((n_ray,)),
+            pltpu.VMEM((n_ray, half // 32, 128), bf16),
+            pltpu.VMEM((32, half // 32, 128), bf16),
+            pltpu.VMEM((8, half // 32, 128), f32),
+            dma((5,)),
+            dma((2,)),
+            dma((1,)),
             dma((n_ray,)),
             dma((2,)),
             dma((2,)),
-            dma((n_ray,)),
-            dma((n_ray,)),
-            dma((n_pair,)),
-            dma((n_pair,)),
-            dma((2,)),
+            dma((1,)),
+            dma((1,)),
+            dma((1,)),
+            dma((1,)),
         ],
         compiler_params=pltpu.CompilerParams(
             collective_id=0, has_side_effects=True, vmem_limit_bytes=56 * 1024 * 1024

time: 45.8 us -> 43.2 us (0.943)
  Pallas kernels: 42.9 us -> 40.3 us
    pallas_call x1, Pallas kernels: 42.9 us -> 40.3 us  [on_device(): pl.pallas_call(functools.partial(kernel, n_ray, n_pix), out_shape=(jax.Sh...]
where the time goes in v2:
time: 43.2 us; the launch traced here: 43.1 us
  Pallas kernels  40.3 us (93%)
  local copies, waits for them, and re-layouts  2.16 us (5%)
  between operations  0.65 us (2%)
    pallas_call x1, Pallas kernels, on_device(): pl.pallas_call(functools.partial(kernel, n_ray, n_pix), out_shape=(jax.Sh...  40.3 us
    unnamed x4, local copies, waits for them, and re-layouts  2.16 us

profile of v2, /device:TPU:1, one launch (start us, length us, event | category | flops | bytes accessed | tf_op | source)
XLA Modules:
  0.0 43.1 jit_solution(5341164458016916892)
XLA Ops:
  0.6 40.3 %ray_wave.1 = (f32[3,64,64]{2,1,0:T(8,128)}, f32[6,1024]{1,0:T(8,128)}) custom-call(f32[2,1024]{1,0:T(2,128)} %pos_hbm.1, f32[2,1024]{1,0:T(2,128)} %dir_hbm.1, f32[1,1024]{1,0:T(1,128)} %bitcast.2, f32[1,1024]{1,0:T(1,128)} %bitcast.3, f32[3,64,64]{2,1,0:T(8,128)} %grad_hbm.1), custom_call_target="tpu_custom_call" | custom-call | tf_op jit(solution)/shard_map/ray_wave/pallas_call | solution.py:449
  40.9 0.0 copy-start
  40.9 1.5 %copy.9 = f32[3,64,64]{2,1,0:T(8,128)} copy(f32[3,64,64]{2,1,0:T(8,128)} %get-tuple-element.4) | data formatting | bytes 98304
  42.5 0.0 copy-done
  42.5 0.6 %copy.10 = f32[6,1024]{1,0:T(8,128)} copy(f32[6,1024]{1,0:T(8,128)S(1)} %copy-done) | data formatting | bytes 49152
Async XLA Ops:
  40.9 1.6 %copy-start = (f32[6,1024]{1,0:T(8,128)S(1)}, f32[6,1024]{1,0:T(8,128)}, u32[]{:S(2)}) copy-start(f32[6,1024]{1,0:T(8,128)} %get-tuple-element.5) | copy-start | bytes 73732

commit v3 on v2

--- a/solution.py
+++ b/solution.py
@@ -98,13 +98,21 @@
     psf_ref,
     out_ref,
     pay,
-    xt,
-    yt,
-    yf,
-    acc,
+    xt0,
+    xt1,
+    xt2,
+    yt0,
+    yt1,
+    yt2,
+    yf0,
+    yf1,
+    yf2,
+    v_loc0,
+    v_loc1,
+    v_loc2,
     g2,
-    v_loc,
     v_rem,
+    power,
     lhs,
     s_snd,
     s_rcv,
@@ -122,6 +130,7 @@
 ):
     me = lax.axis_index("ray")
     pix = lax.axis_index("pix")
+    xt, yt, yf, v_loc = (xt0, xt1, xt2), (yt0, yt1, yt2), (yf0, yf1, yf2), (v_loc0, v_loc1, v_loc2)
     core = pix & 1
     pair = pix >> 1
     x_pos = pair & 3
@@ -203,9 +212,17 @@
         pay_copy(k, me).start()
 
     loads[4].wait()
+    line = lax.broadcasted_iota(jnp.int32, (rows // 2, rows // 2), 0)
+    place = lax.broadcasted_iota(jnp.int32, (rows // 2, rows // 2), 1)
+    flip = (line == core * place + (1 - core) * (rows // 2 - 1 - place)).astype(jnp.float32)
+
+    def exact(left, right, dims):
+        return lax.dot_general(
+            left, right, dims, precision=lax.Precision.HIGHEST, preferred_element_type=jnp.float32
+        )
+
     for wave in range(3):
-        g = grad_ref[wave]
-        g2[core, wave] = jnp.concatenate([g, g], axis=1)
+        g2[core, wave] = exact(grad_ref[wave], flip, (((0,), (0,)), ((), ())))
 
     def g_copy(slot):
         return pltpu.make_async_remote_copy(
@@ -222,114 +239,140 @@
     row_start = pair * rows
     col_start = me * cols
     sub = lax.broadcasted_iota(jnp.int32, (8, half), 0)
-    x_base = (sub + (row_start + rows // 2)).astype(jnp.float32) - (0.5 * NPIX - 0.5)
-    y_base = (sub + (col_start + cols // 2)).astype(jnp.float32) - (0.5 * NPIX - 0.5)
+    x_mid = (row_start + rows // 2).astype(jnp.float32) - 0.5 * NPIX
+    y_mid = (col_start + cols // 2).astype(jnp.float32) - 0.5 * NPIX
+    x_base = sub.astype(jnp.float32) + (0.25 * rows + 0.5)
+    y_base = sub.astype(jnp.float32) + (y_mid + 0.5)
     wave_of = lax.rem(sub, 3)
     step_scale = 8.0 * jnp.where(
         wave_of == 0, wave_scales[0], jnp.where(wave_of == 1, wave_scales[1], wave_scales[2])
     )
 
-    acc[...] = jnp.zeros_like(acc)
-
-    def forward(block):
+    for wave in range(3):
+        v_loc[wave][...] = jnp.zeros_like(v_loc[wave])
+
+    def tables(block):
         rho = jnp.broadcast_to(pay[block, 0:1, :], (8, half))
         l_all = jnp.broadcast_to(pay[block, 1:2, :], (8, half))
         m_all = jnp.broadcast_to(pay[block, 2:3, :], (8, half))
         amp = jnp.broadcast_to(pay[block, 3:4, :], (8, half))
         step_c, step_s = cos_sin_turns(step_scale * jnp.where(sub < 3, l_all, m_all))
-        x_turns = rho + l_all * x_base
-        y_turns = m_all * y_base
-        for wave in range(3):
+        x_turns = l_all * x_base
+        y_turns = (rho + l_all * x_mid) + m_all * y_base
+
+        def row_of(table, index):
+            return jnp.broadcast_to(table[index : index + 1, :], (8, half))
+
+        def one_wave(wave):
             scale = wave_scales[wave]
 
             def store_x(k, first, second):
                 for part in range(2):
                     tile = jnp.concatenate([first[part], second[part]], axis=0)
-                    at = part * rows + 8 * k
-                    xt[wave, block, at : at + 16, :] = tile.astype(jnp.bfloat16)
+                    at = part * (rows // 2) + 8 * k
+                    xt[wave][block, at : at + 16, :] = tile.astype(jnp.bfloat16)
 
             def store_y(k, first, second):
                 for part in range(2):
                     tile = jnp.concatenate([first[part], second[part]], axis=0)
                     at = part * cols + 8 * k
-                    yf[wave, block, at : at + 16, :] = tile
-                    yt[wave, block, at : at + 16, :] = tile.astype(jnp.bfloat16)
-
-            def row_of(table, index):
-                return jnp.broadcast_to(table[index : index + 1, :], (8, half))
-
-            bc, bs = cos_sin_turns(scale * x_turns)
-            ladder((amp * bc, amp * bs), row_of(step_c, wave), row_of(step_s, wave), rows // 8, store_x)
+                    yf[wave][block, at : at + 16, :] = tile
+                    yt[wave][block, at : at + 16, :] = tile.astype(jnp.bfloat16)
+
             ladder(
-                cos_sin_turns(scale * y_turns),
+                cos_sin_turns(scale * x_turns),
+                row_of(step_c, wave),
+                row_of(step_s, wave),
+                rows // 16,
+                store_x,
+            )
+            bc, bs = cos_sin_turns(scale * y_turns)
+            ladder(
+                (amp * bc, amp * bs),
                 row_of(step_c, wave + 3),
                 row_of(step_s, wave + 3),
                 cols // 8,
                 store_y,
             )
-            acc[wave] += lax.dot_general(
-                xt[wave, block],
-                yt[wave, block],
-                (((1,), (1,)), ((), ())),
-                preferred_element_type=jnp.float32,
-            )
-
-    forward(me)
+
+        return one_wave
+
+    def gather_field(block, wave):
+        v_loc[wave][...] += lax.dot_general(
+            yt[wave][block],
+            xt[wave][block],
+            (((1,), (1,)), ((), ())),
+            preferred_element_type=jnp.float32,
+        )
+
+    first = tables(me)
+    first(0)
+    gather_field(me, 0)
+    first(1)
+    gather_field(me, 1)
+    first(2)
 
     def forward_step(k, carry):
+        before = block_of(k - 1)
         block = block_of(k)
         pay_copy(k, block).wait_recv()
-        forward(block)
+        make = tables(block)
+        gather_field(before, 2)
+        make(0)
+        gather_field(block, 0)
+        make(1)
+        gather_field(block, 1)
+        make(2)
         return carry
 
     lax.fori_loop(1, n_ray, forward_step, 0)
-
-    low = lax.broadcasted_iota(jnp.int32, (rows, 2 * cols), 1) < cols
+    gather_field(block_of(n_ray - 1), 2)
+
+    v_copies = [
+        pltpu.make_async_remote_copy(
+            src_ref=v_loc[wave],
+            dst_ref=v_rem.at[wave],
+            send_sem=v_sem.at[0, wave],
+            recv_sem=v_sem.at[1, wave],
+            device_id={"pix": partner},
+            device_id_type=MESH,
+        )
+        for wave in range(3)
+    ]
+    for v_copy in v_copies:
+        v_copy.start()
+    g_copy(1 - core).wait_recv()
+
+    low = lax.broadcasted_iota(jnp.int32, (cols, rows), 1) < rows // 2
+    distance = (lax.broadcasted_iota(jnp.int32, (cols, rows), 1) & (rows // 2 - 1)).astype(
+        jnp.float32
+    ) + 0.5
+
+    def swap(a):
+        return pltpu.roll(a, rows // 2, 1)
+
     for wave in range(3):
-        other = acc[wave, rows : 2 * rows, :]
-        v_loc[wave] = acc[wave, 0:rows, :] + pltpu.roll(jnp.where(low, other, -other), cols, 1)
-
-    v_copy = pltpu.make_async_remote_copy(
-        src_ref=v_loc,
-        dst_ref=v_rem,
-        send_sem=v_sem.at[0],
-        recv_sem=v_sem.at[1],
-        device_id={"pix": partner},
-        device_id_type=MESH,
-    )
-    v_copy.start()
-    g_copy(1 - core).wait_recv()
-    v_copy.wait_recv()
-
-    own_rows = pl.ds(pl.multiple_of(core * (rows // 2), 8), rows // 2)
-    offset = (lax.broadcasted_iota(jnp.int32, (2 * cols // 2, rows), 1)).astype(jnp.float32) - (
-        0.5 * rows - 0.5
-    )
-    for wave in range(3):
-        own = v_loc[wave, own_rows, :] + v_rem[wave, own_rows, :]
-        power = own * own
-        psf_ref[wave] = (power + pltpu.roll(power, cols, 1))[:, :cols]
-        field = v_loc[wave] + v_rem[wave]
-        weight = jnp.concatenate([g2[0, wave], g2[1, wave]], axis=0)
-        grad_t = jnp.transpose(2.0 * weight * field)
-        re = grad_t[:cols]
-        im = grad_t[cols:]
-        lhs[wave, 0:cols, 0:rows] = re.astype(jnp.bfloat16)
-        lhs[wave, 0:cols, rows:] = im.astype(jnp.bfloat16)
-        lhs[wave, cols : 2 * cols, 0:rows] = im.astype(jnp.bfloat16)
-        lhs[wave, cols : 2 * cols, rows:] = (-re).astype(jnp.bfloat16)
-        re = re * offset
-        im = im * offset
-        lhs[wave, 2 * cols : 3 * cols, 0:rows] = re.astype(jnp.bfloat16)
-        lhs[wave, 2 * cols : 3 * cols, rows:] = im.astype(jnp.bfloat16)
-        lhs[wave, 3 * cols :, 0:rows] = im.astype(jnp.bfloat16)
-        lhs[wave, 3 * cols :, rows:] = (-re).astype(jnp.bfloat16)
-
-    psf_store = pltpu.make_async_copy(psf_ref, psf_hbm, out_sem.at[0])
-    psf_store.start()
-
-    x_mid = (row_start + rows // 2).astype(jnp.float32) - 0.5 * NPIX
-    y_mid = (col_start + cols // 2).astype(jnp.float32) - 0.5 * NPIX
+        v_copies[wave].wait_recv()
+        top = v_loc[wave][0:cols, :] + v_rem[wave, 0:cols, :]
+        bot = v_loc[wave][cols:, :] + v_rem[wave, cols:, :]
+        top_s, bot_s = swap(top), swap(bot)
+        u_re = jnp.where(low, top - bot_s, top_s + bot)
+        u_im = jnp.where(low, bot + top_s, bot_s - top)
+        power[wave] = u_re * u_re + u_im * u_im
+        weight = 2.0 * jnp.concatenate([g2[1, wave], g2[0, wave]], axis=1)
+        g_re, g_im = weight * u_re, weight * u_im
+        r_re, r_im = swap(g_re), swap(g_im)
+        plus_re, less_re = g_re + r_re, g_re - r_re
+        plus_im, less_im = g_im + r_im, g_im - r_im
+        for i, table in enumerate(
+            (
+                jnp.where(low, plus_re, -less_im),
+                jnp.where(low, plus_im, less_re),
+                jnp.where(low, less_re, plus_im) * distance,
+                jnp.where(low, less_im, -plus_re) * distance,
+            )
+        ):
+            lhs[wave, i * cols : (i + 1) * cols, :] = table.astype(jnp.bfloat16)
 
     here = 8 * y_pos + z_pos
 
@@ -353,7 +396,7 @@
         for wave in range(3):
             d_b = lax.dot_general(
                 lhs[wave],
-                xt[wave, block],
+                xt[wave][block],
                 (((1,), (0,)), ((), ())),
                 preferred_element_type=jnp.float32,
             )
@@ -362,8 +405,8 @@
             zy = jnp.zeros((8, half), jnp.float32)
             for t in range(cols // 8):
                 at = 8 * t
-                br = yf[wave, block, at : at + 8, :]
-                bi = yf[wave, block, cols + at : cols + at + 8, :]
+                br = yf[wave][block, at : at + 8, :]
+                bi = yf[wave][block, cols + at : cols + at + 8, :]
                 dbr = d_b[at : at + 8]
                 dbi = d_b[cols + at : cols + at + 8]
                 dxr = d_b[2 * cols + at : 2 * cols + at + 8]
@@ -383,17 +426,23 @@
         )
 
     def backward_step(i, carry):
-        k = n_ray - i
+        k = 4 * (3 - (i & 3)) + (i >> 2)
         s_snd[k] = backward(block_of(k)).astype(jnp.bfloat16)
         s_copy(k, 1).start()
-        s_copy(k, 0).start()
+
+        @pl.when(k > 0)
+        def _():
+            s_copy(k, 0).start()
+
         return carry
 
-    lax.fori_loop(1, n_ray, backward_step, 0)
-    s_own = backward(me).astype(jnp.bfloat16)
-    s_snd[0] = s_own
-    s_copy(0, 1).start()
-    s_rcv[here] = s_own
+    lax.fori_loop(0, n_ray, backward_step, 0)
+    s_rcv[here] = s_snd[0]
+    for wave in range(3):
+        above, below = power[wave, :, : rows // 2], power[wave, :, rows // 2 :]
+        psf_ref[wave] = exact(flip, jnp.where(core == 1, above, below), (((1,), (1,)), ((), ())))
+    psf_store = pltpu.make_async_copy(psf_ref, psf_hbm, out_sem.at[0])
+    psf_store.start()
     wait_bytes(s_rcv.at[0:31], s_recv.at[0])
     total = s_rcv[0].astype(jnp.float32)
     for b in range(1, 32):
@@ -431,7 +480,8 @@
     wait_bytes(s_rcv.at[0:31], s_send.at[0])
     wait_bytes(tot.at[0:7], t_send.at[0])
     g_copy(core).wait_send()
-    v_copy.wait_send()
+    for v_copy in v_copies:
+        v_copy.wait_send()
     psf_store.wait()
     out_store.wait()
 
@@ -444,6 +494,7 @@
     cols = NPIX // n_ray
     f32 = jnp.float32
     bf16 = jnp.bfloat16
+    hbm_space = pl.BlockSpec(memory_space=pltpu.HBM)
     any_space = pl.BlockSpec(memory_space=pl.ANY)
     dma = pltpu.SemaphoreType.DMA
     return pl.pallas_call(
@@ -452,7 +503,7 @@
             jax.ShapeDtypeStruct(psf_grad.shape, f32),
             jax.ShapeDtypeStruct((6, count), f32),
         ),
-        in_specs=[any_space] * 5,
+        in_specs=[hbm_space] * 5,
         out_specs=(any_space, any_space),
         scratch_shapes=[
             pltpu.VMEM((2, count), f32),
@@ -463,14 +514,14 @@
             pltpu.VMEM(psf_grad.shape, f32),
             pltpu.VMEM((6, count), f32),
             pltpu.VMEM((n_ray, 4, half), f32),
-            pltpu.VMEM((3, n_ray, 2 * rows, half), bf16),
-            pltpu.VMEM((3, n_ray, 2 * cols, half), bf16),
-            pltpu.VMEM((3, n_ray, 2 * cols, half), f32),
-            pltpu.VMEM((3, 2 * rows, 2 * cols), f32),
-            pltpu.VMEM((2, 3, rows // 2, 2 * cols), f32),
-            pltpu.VMEM((3, rows, 2 * cols), f32),
-            pltpu.VMEM((3, rows, 2 * cols), f32),
-            pltpu.VMEM((3, 4 * cols, 2 * rows), bf16),
+            *[pltpu.VMEM((n_ray, rows, half), bf16)] * 3,
+            *[pltpu.VMEM((n_ray, 2 * cols, half), bf16)] * 3,
+            *[pltpu.VMEM((n_ray, 2 * cols, half), f32)] * 3,
+            *[pltpu.VMEM((2 * cols, rows), f32)] * 3,
+            pltpu.VMEM((2, 3, cols, rows // 2), f32),
+            pltpu.VMEM((3, 2 * cols, rows), f32),
+            pltpu.VMEM((3, cols, rows), f32),
+            pltpu.VMEM((3, 4 * cols, rows), bf16),
             pltpu.VMEM((n_ray, half // 32, 128), bf16),
             pltpu.VMEM((32, half // 32, 128), bf16),
             pltpu.VMEM((8, half // 32, 128), f32),
@@ -479,14 +530,14 @@
             dma((1,)),
             dma((n_ray,)),
             dma((2,)),
-            dma((2,)),
+            dma((2, 3)),
             dma((1,)),
             dma((1,)),
             dma((1,)),
             dma((1,)),
         ],
         compiler_params=pltpu.CompilerParams(
-            collective_id=0, has_side_effects=True, vmem_limit_bytes=56 * 1024 * 1024
+            collective_id=0, has_side_effects=True, vmem_limit_bytes=48 * 1024 * 1024
         ),
         name="ray_wave",
     )(positions, directions, path.reshape(1, count), amplitude.reshape(1, count), psf_grad)

time: 43.2 us -> 42.6 us (0.986)
  Pallas kernels: 40.3 us -> 36.8 us
  local copies, waits for them, and re-layouts: 2.16 us -> 4.91 us
    pallas_call x1, Pallas kernels: 40.3 us -> 36.8 us  [on_device(): pl.pallas_call(functools.partial(kernel, n_ray, n_pix), out_shape=(jax.Sh...]
    unnamed x4 -> x12, local copies, waits for them, and re-layouts: 2.16 us -> 4.91 us
where the time goes in v3:
time: 42.6 us; the launch traced here: 42.3 us
  Pallas kernels  36.8 us (86%)
  local copies, waits for them, and re-layouts  4.91 us (12%)
  between operations  0.65 us (2%)
    pallas_call x1, Pallas kernels, on_device(): pl.pallas_call(functools.partial(kernel, n_ray, n_pix), out_shape=(jax.Sh...  36.8 us
    unnamed x12, local copies, waits for them, and re-layouts  4.91 us

profile of v3, /device:TPU:1, one launch (start us, length us, event | category | flops | bytes accessed | tf_op | source)
XLA Modules:
  0.0 42.3 jit_solution(4654050597096255601)
XLA Ops:
  0.6 0.0 copy-start
  0.6 0.9 %copy-done = f32[3,64,64]{2,1,0:T(8,128)S(1)} copy-done((f32[3,64,64]{2,1,0:T(8,128)S(1)}, f32[3,64,64]{2,1,0:T(8,128)}, u32[]{:S(2)}) %copy-start) | copy-done | bytes 49176
  1.5 0.0 copy-start.1
  1.5 0.7 %copy-done.1 = f32[2,1024]{1,0:T(2,128)S(1)} copy-done((f32[2,1024]{1,0:T(2,128)S(1)}, f32[2,1024]{1,0:T(2,128)}, u32[]{:S(2)}) %copy-start.1) | copy-done | bytes 8216
  2.2 0.0 copy-start.2
  2.2 0.7 %copy-done.2 = f32[2,1024]{1,0:T(2,128)S(1)} copy-done((f32[2,1024]{1,0:T(2,128)S(1)}, f32[2,1024]{1,0:T(2,128)}, u32[]{:S(2)}) %copy-start.2) | copy-done | bytes 8216
  2.9 0.0 copy-start.3
  2.9 0.7 %copy-done.3 = f32[1024]{0:T(1024)S(1)} copy-done((f32[1024]{0:T(1024)S(1)}, f32[1024]{0:T(1024)}, u32[]{:S(2)}) %copy-start.3) | copy-done | bytes 4120
  3.6 0.0 copy-start.4
  3.6 0.7 %copy-done.4 = f32[1024]{0:T(1024)S(1)} copy-done((f32[1024]{0:T(1024)S(1)}, f32[1024]{0:T(1024)}, u32[]{:S(2)}) %copy-start.4) | copy-done | bytes 4120
  4.3 36.8 %ray_wave.1 = (f32[3,64,64]{2,1,0:T(8,128)S(1)}, f32[6,1024]{1,0:T(8,128)S(1)}) custom-call(f32[2,1024]{1,0:T(2,128)S(1)} %copy-done.1, f32[2,1024]{1,0:T(2,128)S(1)} %copy-done.2, f32[1,1024]{1,0:T(1,128)S(1)} %bitcast.2, f32[1,1024]{1,0:T(1,128)S(1)} %bitcast.3, f32[3,64,64]{2,1,0:T(8,128)S(1)} %copy-done), custom_call_target="tpu_custom_call" | custom-call | tf_op jit(solution)/shard_map/ray_wave/pallas_call | solution.py:500
  41.1 0.6 %copy.9 = f32[3,64,64]{2,1,0:T(8,128)} copy(f32[3,64,64]{2,1,0:T(8,128)S(1)} %get-tuple-element.4) | data formatting | bytes 98304
  41.7 0.6 %copy.10 = f32[6,1024]{1,0:T(8,128)} copy(f32[6,1024]{1,0:T(8,128)S(1)} %get-tuple-element.5) | data formatting | bytes 49152
Async XLA Ops:
  0.6 0.9 %copy-start = (f32[3,64,64]{2,1,0:T(8,128)S(1)}, f32[3,64,64]{2,1,0:T(8,128)}, u32[]{:S(2)}) copy-start(f32[3,64,64]{2,1,0:T(8,128)} %grad_hbm.1) | copy-start | bytes 147460
  1.5 0.7 %copy-start.1 = (f32[2,1024]{1,0:T(2,128)S(1)}, f32[2,1024]{1,0:T(2,128)}, u32[]{:S(2)}) copy-start(f32[2,1024]{1,0:T(2,128)} %pos_hbm.1) | copy-start | bytes 24580
  2.2 0.7 %copy-start.2 = (f32[2,1024]{1,0:T(2,128)S(1)}, f32[2,1024]{1,0:T(2,128)}, u32[]{:S(2)}) copy-start(f32[2,1024]{1,0:T(2,128)} %dir_hbm.1) | copy-start | bytes 24580
  2.9 0.7 %copy-start.3 = (f32[1024]{0:T(1024)S(1)}, f32[1024]{0:T(1024)}, u32[]{:S(2)}) copy-start(f32[1024]{0:T(1024)} %param.7) | copy-start | bytes 12292
  3.6 0.7 %copy-start.4 = (f32[1024]{0:T(1024)S(1)}, f32[1024]{0:T(1024)}, u32[]{:S(2)}) copy-start(f32[1024]{0:T(1024)} %param.8) | copy-start | bytes 12292

commit v4 on v3

--- a/solution.py
+++ b/solution.py
@@ -306,27 +306,23 @@
         )
 
     first = tables(me)
-    first(0)
-    gather_field(me, 0)
-    first(1)
-    gather_field(me, 1)
-    first(2)
+    for wave in range(3):
+        first(wave)
 
     def forward_step(k, carry):
         before = block_of(k - 1)
         block = block_of(k)
         pay_copy(k, block).wait_recv()
         make = tables(block)
-        gather_field(before, 2)
-        make(0)
-        gather_field(block, 0)
-        make(1)
-        gather_field(block, 1)
-        make(2)
+        for wave in range(3):
+            gather_field(before, wave)
+        for wave in range(3):
+            make(wave)
         return carry
 
     lax.fori_loop(1, n_ray, forward_step, 0)
-    gather_field(block_of(n_ray - 1), 2)
+    for wave in range(3):
+        gather_field(block_of(n_ray - 1), wave)
 
     v_copies = [
         pltpu.make_async_remote_copy(
@@ -540,7 +536,10 @@
             collective_id=0, has_side_effects=True, vmem_limit_bytes=48 * 1024 * 1024
         ),
         name="ray_wave",
-    )(positions, directions, path.reshape(1, count), amplitude.reshape(1, count), psf_grad)
+    )(*[
+        pltpu.with_memory_space_constraint(v, pltpu.HBM)
+        for v in (positions, directions, path.reshape(1, count), amplitude.reshape(1, count), psf_grad)
+    ])
 
 
 def solution(mesh):

time: 42.6 us -> 37.6 us (0.88)
  local copies, waits for them, and re-layouts: 4.91 us -> 1.26 us
  Pallas kernels: 36.8 us -> 35.5 us
    unnamed x12 -> x2, local copies, waits for them, and re-layouts: 4.91 us -> 1.26 us
    pallas_call x1, Pallas kernels: 36.8 us -> 35.5 us  [on_device(): pl.pallas_call(functools.partial(kernel, n_ray, n_pix), out_shape=(jax.Sh...]
where the time goes in v4:
time: 37.6 us; the launch traced here: 37.4 us
  Pallas kernels  35.5 us (94%)
  local copies, waits for them, and re-layouts  1.26 us (3%)
  between operations  0.64 us (2%)
    pallas_call x1, Pallas kernels, on_device(): pl.pallas_call(functools.partial(kernel, n_ray, n_pix), out_shape=(jax.Sh...  35.5 us
    unnamed x2, local copies, waits for them, and re-layouts  1.26 us

profile of v4, /device:TPU:1, one launch (start us, length us, event | category | flops | bytes accessed | tf_op | source)
XLA Modules:
  0.0 37.4 jit_solution(10008766162051693614)
XLA Ops:
  0.6 35.5 %ray_wave.1 = (f32[3,64,64]{2,1,0:T(8,128)S(1)}, f32[6,1024]{1,0:T(8,128)S(1)}) custom-call(f32[2,1024]{1,0:T(2,128)} %pos_hbm.1, f32[2,1024]{1,0:T(2,128)} %dir_hbm.1, f32[1,1024]{1,0:T(1,128)} %bitcast.2, f32[1,1024]{1,0:T(1,128)} %bitcast.3, f32[3,64,64]{2,1,0:T(8,128)} %grad_hbm.1), custom_call_target="tpu_custom_call" | custom-call | tf_op jit(solution)/shard_map/ray_wave/pallas_call | solution.py:496
  36.2 0.6 %copy.9 = f32[3,64,64]{2,1,0:T(8,128)} copy(f32[3,64,64]{2,1,0:T(8,128)S(1)} %get-tuple-element.4) | data formatting | bytes 98304
  36.8 0.6 %copy.10 = f32[6,1024]{1,0:T(8,128)} copy(f32[6,1024]{1,0:T(8,128)S(1)} %get-tuple-element.5) | data formatting | bytes 49152

commit v5 on v4

--- a/solution.py
+++ b/solution.py
@@ -78,6 +78,10 @@
     dy = b + (b >> 1) - 2 * b3
     dz = a + 5 * (a >> 1) - 6 * a3 + 4 * a3 * (dy & 1)
     return dy, dz
+
+
+def fold_row(j):
+    return 8 * (j & 1) + 4 * (j >> 3 & 1) + 2 * (j >> 2 & 1) + (j >> 1 & 1)
 
 
 def kernel(
@@ -176,7 +180,8 @@
     def x_peer(dx, other):
         return {"pix": (pix & 8) + 2 * ((x_pos + dx) & 3) + (core + other - 2 * core * other)}
 
-    x_others = [(dx, other) for dx in range(4) for other in range(2)][1:]
+    x_others = [(dx, other) for dx in (2, 1, 3, 0) for other in range(2)][:7]
+    x_others[6] = (0, 1)
 
     for dy, dz in [(dy, dz) for dy in range(4) for dz in (0, 1, 7, 2, 6)][1:]:
         pl.semaphore_signal(barrier, inc=1, device_id=chip_at(dy, dz), device_id_type=MESH)
@@ -297,33 +302,31 @@
 
         return one_wave
 
-    def gather_field(block, wave):
-        v_loc[wave][...] += lax.dot_general(
+    def gather_field(block, wave, keep):
+        total = v_loc[wave][...] + lax.dot_general(
             yt[wave][block],
             xt[wave][block],
             (((1,), (1,)), ((), ())),
             preferred_element_type=jnp.float32,
         )
-
-    first = tables(me)
-    for wave in range(3):
-        first(wave)
+        v_loc[wave][...] = jnp.where(keep, total, 0.0)
 
     def forward_step(k, carry):
-        before = block_of(k - 1)
+        before = block_of((k - 1) & (n_ray - 1))
         block = block_of(k)
-        pay_copy(k, block).wait_recv()
+
+        @pl.when(k > 0)
+        def _():
+            pay_copy(k, block).wait_recv()
+
         make = tables(block)
         for wave in range(3):
-            gather_field(before, wave)
+            gather_field(before, wave, k > 0)
         for wave in range(3):
             make(wave)
         return carry
 
-    lax.fori_loop(1, n_ray, forward_step, 0)
-    for wave in range(3):
-        gather_field(block_of(n_ray - 1), wave)
-
+    lax.fori_loop(0, n_ray, forward_step, 0)
     v_copies = [
         pltpu.make_async_remote_copy(
             src_ref=v_loc[wave],
@@ -335,8 +338,9 @@
         )
         for wave in range(3)
     ]
-    for v_copy in v_copies:
-        v_copy.start()
+    for wave in range(3):
+        gather_field(block_of(n_ray - 1), wave, True)
+        v_copies[wave].start()
     g_copy(1 - core).wait_recv()
 
     low = lax.broadcasted_iota(jnp.int32, (cols, rows), 1) < rows // 2
@@ -383,56 +387,76 @@
             device_id_type=MESH,
         )
 
-    def backward(block):
-        s1 = jnp.zeros((8, half), jnp.float32)
-        s2 = jnp.zeros((8, half), jnp.float32)
-        s3 = jnp.zeros((8, half), jnp.float32)
-        s4 = jnp.zeros((8, half), jnp.float32)
-        sub_f = sub.astype(jnp.float32)
+    def project(block, wave):
+        return lax.dot_general(
+            lhs[wave],
+            xt[wave][block],
+            (((1,), (0,)), ((), ())),
+            preferred_element_type=jnp.float32,
+        )
+
+    sub_f = sub.astype(jnp.float32)
+
+    def contract(block, wave, sums):
+        d_wave = project(block, wave)
+        s1, s2, s3, s4 = sums
+        zi = zx = zy = None
+        for t in range(cols // 8):
+            at = 8 * t
+            br = yf[wave][block, at : at + 8, :]
+            bi = yf[wave][block, cols + at : cols + at + 8, :]
+            dbr = d_wave[at : at + 8, :]
+            dbi = d_wave[cols + at : cols + at + 8, :]
+            dxr = d_wave[2 * cols + at : 2 * cols + at + 8, :]
+            dxi = d_wave[3 * cols + at : 3 * cols + at + 8, :]
+            d = br * dbi - bi * dbr
+            dx = br * dxi - bi * dxr
+            dy = d * (sub_f + (at - 0.5 * cols + 0.5))
+            s4 = s4 + (br * dbr + bi * dbi)
+            zi, zx, zy = (d, dx, dy) if t == 0 else (zi + d, zx + dx, zy + dy)
+        scale = wave_scales[wave]
+        s1 = s1 + scale * zi
+        s2 = s2 + (scale * two_pi) * (x_mid * zi + zx)
+        s3 = s3 + (scale * two_pi) * (y_mid * zi + zy)
+        return s1, s2, s3, s4
+
+    def order(i):
+        a = (i >> 2) & 3
+        return 4 * ((3 + ((4 - a) >> 2) - (i & 3)) & 3) + a
+
+    def fold(tiles):
+        lane_row = lax.broadcasted_iota(jnp.int32, (8, 128), 0)
+        for shift in (4, 2, 1):
+            keep = (lane_row & shift) == 0
+            n = len(tiles) // 2
+            tiles = [
+                jnp.where(keep, a + pltpu.roll(a, 8 - shift, 0), b + pltpu.roll(b, shift, 0))
+                for a, b in zip(tiles[:n], tiles[n:])
+            ]
+        return jnp.concatenate(tiles, axis=0)
+
+    def one_block(k, block):
+        sums = (jnp.zeros((8, half), jnp.float32),) * 4
         for wave in range(3):
-            d_b = lax.dot_general(
-                lhs[wave],
-                xt[wave][block],
-                (((1,), (0,)), ((), ())),
-                preferred_element_type=jnp.float32,
-            )
-            zi = jnp.zeros((8, half), jnp.float32)
-            zx = jnp.zeros((8, half), jnp.float32)
-            zy = jnp.zeros((8, half), jnp.float32)
-            for t in range(cols // 8):
-                at = 8 * t
-                br = yf[wave][block, at : at + 8, :]
-                bi = yf[wave][block, cols + at : cols + at + 8, :]
-                dbr = d_b[at : at + 8]
-                dbi = d_b[cols + at : cols + at + 8]
-                dxr = d_b[2 * cols + at : 2 * cols + at + 8]
-                dxi = d_b[3 * cols + at : 3 * cols + at + 8]
-                d = br * dbi - bi * dbr
-                zi = zi + d
-                zy = zy + d * (sub_f + (at - 0.5 * cols + 0.5))
-                zx = zx + (br * dxi - bi * dxr)
-                s4 = s4 + (br * dbr + bi * dbi)
-            scale = wave_scales[wave]
-            s1 = s1 + scale * zi
-            s2 = s2 + (scale * two_pi) * (x_mid * zi + zx)
-            s3 = s3 + (scale * two_pi) * (y_mid * zi + zy)
-        sums = [jnp.sum(s, axis=0, keepdims=True) for s in (s1, s2, s3, s4)]
-        return jnp.concatenate(
-            [s[:, 128 * t : 128 * t + 128] for s in sums for t in range(half // 128)], axis=0
-        )
+            sums = contract(block, wave, sums)
+        tiles = [s[:, 128 * t : 128 * t + 128] for s in sums for t in range(half // 128)]
+        s_snd[k] = fold(tiles).astype(jnp.bfloat16)
 
     def backward_step(i, carry):
-        k = 4 * (3 - (i & 3)) + (i >> 2)
-        s_snd[k] = backward(block_of(k)).astype(jnp.bfloat16)
-        s_copy(k, 1).start()
-
-        @pl.when(k > 0)
+        ks = [order(2 * i + n) for n in range(2)]
+        for k in ks:
+            one_block(k, block_of(k))
+        for k in ks:
+            s_copy(k, 1).start()
+
+        @pl.when(i > 0)
         def _():
-            s_copy(k, 0).start()
-
+            s_copy(ks[0], 0).start()
+
+        s_copy(ks[1], 0).start()
         return carry
 
-    lax.fori_loop(0, n_ray, backward_step, 0)
+    lax.fori_loop(0, n_ray // 2, backward_step, 0)
     s_rcv[here] = s_snd[0]
     for wave in range(3):
         above, below = power[wave, :, : rows // 2], power[wave, :, rows // 2 :]
@@ -462,7 +486,7 @@
             total = total + tot[4 * h + b]
         for t in range(tiles):
             at = slice(h * half + 128 * t, h * half + 128 * t + 128)
-            s1, s2, s3, s4 = (total[tiles * i + t : tiles * i + t + 1] for i in range(4))
+            s1, s2, s3, s4 = (total[r : r + 1] for r in (fold_row(tiles * i + t) for i in range(4)))
             out_ref[0:1, at] = s1
             out_ref[1:2, at] = -two_pi * dir_ref[0:1, at] * s1
             out_ref[2:3, at] = -two_pi * dir_ref[1:2, at] * s1

time: 37.6 us -> 36.9 us (0.981)
  Pallas kernels: 35.5 us -> 34.8 us
    pallas_call x1, Pallas kernels: 35.5 us -> 34.8 us  [on_device(): pl.pallas_call(functools.partial(kernel, n_ray, n_pix), out_shape=(jax.Sh...]
where the time goes in v5:
time: 36.9 us; the launch traced here: 36.7 us
  Pallas kernels  34.8 us (94%)
  local copies, waits for them, and re-layouts  1.26 us (3%)
  between operations  0.64 us (2%)
    pallas_call x1, Pallas kernels, on_device(): pl.pallas_call(functools.partial(kernel, n_ray, n_pix), out_shape=(jax.Sh...  34.8 us
    unnamed x2, local copies, waits for them, and re-layouts  1.26 us

profile of v5, /device:TPU:1, one launch (start us, length us, event | category | flops | bytes accessed | tf_op | source)
XLA Modules:
  0.0 36.7 jit_solution(14117875572054250517)
XLA Ops:
  0.6 34.8 %ray_wave.1 = (f32[3,64,64]{2,1,0:T(8,128)S(1)}, f32[6,1024]{1,0:T(8,128)S(1)}) custom-call(f32[2,1024]{1,0:T(2,128)} %pos_hbm.1, f32[2,1024]{1,0:T(2,128)} %dir_hbm.1, f32[1,1024]{1,0:T(1,128)} %bitcast.2, f32[1,1024]{1,0:T(1,128)} %bitcast.3, f32[3,64,64]{2,1,0:T(8,128)} %grad_hbm.1), custom_call_target="tpu_custom_call" | custom-call | tf_op jit(solution)/shard_map/ray_wave/pallas_call | solution.py:520
  35.5 0.6 %copy.9 = f32[3,64,64]{2,1,0:T(8,128)} copy(f32[3,64,64]{2,1,0:T(8,128)S(1)} %get-tuple-element.4) | data formatting | bytes 98304
  36.1 0.6 %copy.10 = f32[6,1024]{1,0:T(8,128)} copy(f32[6,1024]{1,0:T(8,128)S(1)} %get-tuple-element.5) | data formatting | bytes 49152

commit v6 on v5

--- a/solution.py
+++ b/solution.py
@@ -183,7 +183,7 @@
     x_others = [(dx, other) for dx in (2, 1, 3, 0) for other in range(2)][:7]
     x_others[6] = (0, 1)
 
-    for dy, dz in [(dy, dz) for dy in range(4) for dz in (0, 1, 7, 2, 6)][1:]:
+    for dy, dz in ((2, 2), (2, 6), (1, 2), (1, 6), (2, 1), (2, 7), (3, 2), (3, 6), (0, 2), (0, 6), (1, 1), (1, 7), (2, 0), (3, 1), (3, 7), (0, 1), (0, 7), (1, 0), (3, 0)):
         pl.semaphore_signal(barrier, inc=1, device_id=chip_at(dy, dz), device_id_type=MESH)
     for dx, other in x_others:
         pl.semaphore_signal(barrier, inc=1, device_id=x_peer(dx, other), device_id_type=MESH)

time: 36.9 us -> 36.8 us (level)
  no operation moved by 1% of the time
where the time goes in v6:
time: 36.8 us; the launch traced here: 36.6 us
  Pallas kernels  34.7 us (94%)
  local copies, waits for them, and re-layouts  1.26 us (3%)
  between operations  0.64 us (2%)
    pallas_call x1, Pallas kernels, on_device(): pl.pallas_call(functools.partial(kernel, n_ray, n_pix), out_shape=(jax.Sh...  34.7 us
    unnamed x2, local copies, waits for them, and re-layouts  1.26 us

profile of v6, /device:TPU:1, one launch (start us, length us, event | category | flops | bytes accessed | tf_op | source)
XLA Modules:
  0.0 36.6 jit_solution(683289795796625623)
XLA Ops:
  0.6 34.7 %ray_wave.1 = (f32[3,64,64]{2,1,0:T(8,128)S(1)}, f32[6,1024]{1,0:T(8,128)S(1)}) custom-call(f32[2,1024]{1,0:T(2,128)} %pos_hbm.1, f32[2,1024]{1,0:T(2,128)} %dir_hbm.1, f32[1,1024]{1,0:T(1,128)} %bitcast.2, f32[1,1024]{1,0:T(1,128)} %bitcast.3, f32[3,64,64]{2,1,0:T(8,128)} %grad_hbm.1), custom_call_target="tpu_custom_call" | custom-call | tf_op jit(solution)/shard_map/ray_wave/pallas_call | solution.py:520
  35.4 0.6 %copy.9 = f32[3,64,64]{2,1,0:T(8,128)} copy(f32[3,64,64]{2,1,0:T(8,128)S(1)} %get-tuple-element.4) | data formatting | bytes 98304
  36.0 0.6 %copy.10 = f32[6,1024]{1,0:T(8,128)} copy(f32[6,1024]{1,0:T(8,128)S(1)} %get-tuple-element.5) | data formatting | bytes 49152

commit v7 on v5

--- a/solution.py
+++ b/solution.py
@@ -458,11 +458,6 @@
 
     lax.fori_loop(0, n_ray // 2, backward_step, 0)
     s_rcv[here] = s_snd[0]
-    for wave in range(3):
-        above, below = power[wave, :, : rows // 2], power[wave, :, rows // 2 :]
-        psf_ref[wave] = exact(flip, jnp.where(core == 1, above, below), (((1,), (1,)), ((), ())))
-    psf_store = pltpu.make_async_copy(psf_ref, psf_hbm, out_sem.at[0])
-    psf_store.start()
     wait_bytes(s_rcv.at[0:31], s_recv.at[0])
     total = s_rcv[0].astype(jnp.float32)
     for b in range(1, 32):
@@ -478,6 +473,11 @@
             device_id=x_peer(dx, other),
             device_id_type=MESH,
         ).start()
+    for wave in range(3):
+        above, below = power[wave, :, : rows // 2], power[wave, :, rows // 2 :]
+        psf_ref[wave] = exact(flip, jnp.where(core == 1, above, below), (((1,), (1,)), ((), ())))
+    psf_store = pltpu.make_async_copy(psf_ref, psf_hbm, out_sem.at[0])
+    psf_store.start()
     wait_bytes(tot.at[0:7], t_recv.at[0])
     tiles = half // 128
     for h in range(2):

time: 36.9 us -> 36.9 us (level)
  no operation moved by 1% of the time
where the time goes in v7:
time: 36.9 us; the launch traced here: 36.7 us
  Pallas kernels  34.8 us (94%)
  local copies, waits for them, and re-layouts  1.26 us (3%)
  between operations  0.64 us (2%)
    pallas_call x1, Pallas kernels, on_device(): pl.pallas_call(functools.partial(kernel, n_ray, n_pix), out_shape=(jax.Sh...  34.8 us
    unnamed x2, local copies, waits for them, and re-layouts  1.26 us

profile of v7, /device:TPU:1, one launch (start us, length us, event | category | flops | bytes accessed | tf_op | source)
XLA Modules:
  0.0 36.7 jit_solution(18341947011545920264)
XLA Ops:
  0.6 34.8 %ray_wave.1 = (f32[3,64,64]{2,1,0:T(8,128)S(1)}, f32[6,1024]{1,0:T(8,128)S(1)}) custom-call(f32[2,1024]{1,0:T(2,128)} %pos_hbm.1, f32[2,1024]{1,0:T(2,128)} %dir_hbm.1, f32[1,1024]{1,0:T(1,128)} %bitcast.2, f32[1,1024]{1,0:T(1,128)} %bitcast.3, f32[3,64,64]{2,1,0:T(8,128)} %grad_hbm.1), custom_call_target="tpu_custom_call" | custom-call | tf_op jit(solution)/shard_map/ray_wave/pallas_call | solution.py:520
  35.5 0.6 %copy.9 = f32[3,64,64]{2,1,0:T(8,128)} copy(f32[3,64,64]{2,1,0:T(8,128)S(1)} %get-tuple-element.4) | data formatting | bytes 98304
  36.1 0.6 %copy.10 = f32[6,1024]{1,0:T(8,128)} copy(f32[6,1024]{1,0:T(8,128)S(1)} %get-tuple-element.5) | data formatting | bytes 49152

commit v8 on v7

--- a/solution.py
+++ b/solution.py
@@ -183,7 +183,7 @@
     x_others = [(dx, other) for dx in (2, 1, 3, 0) for other in range(2)][:7]
     x_others[6] = (0, 1)
 
-    for dy, dz in [(dy, dz) for dy in range(4) for dz in (0, 1, 7, 2, 6)][1:]:
+    for dy, dz in ((2, 2), (2, 6), (1, 2), (1, 6), (2, 1), (2, 7), (3, 2), (3, 6), (0, 2), (0, 6), (1, 1), (1, 7), (2, 0), (3, 1), (3, 7), (0, 1), (0, 7), (1, 0), (3, 0)):
         pl.semaphore_signal(barrier, inc=1, device_id=chip_at(dy, dz), device_id_type=MESH)
     for dx, other in x_others:
         pl.semaphore_signal(barrier, inc=1, device_id=x_peer(dx, other), device_id_type=MESH)

time: 36.9 us -> 36.8 us (level)
  no operation moved by 1% of the time
where the time goes in v8:
time: 36.8 us; the launch traced here: 36.6 us
  Pallas kernels  34.7 us (94%)
  local copies, waits for them, and re-layouts  1.26 us (3%)
  between operations  0.64 us (2%)
    pallas_call x1, Pallas kernels, on_device(): pl.pallas_call(functools.partial(kernel, n_ray, n_pix), out_shape=(jax.Sh...  34.7 us
    unnamed x2, local copies, waits for them, and re-layouts  1.26 us

profile of v8, /device:TPU:1, one launch (start us, length us, event | category | flops | bytes accessed | tf_op | source)
XLA Modules:
  0.0 36.6 jit_solution(1817038716456006028)
XLA Ops:
  0.6 34.7 %ray_wave.1 = (f32[3,64,64]{2,1,0:T(8,128)S(1)}, f32[6,1024]{1,0:T(8,128)S(1)}) custom-call(f32[2,1024]{1,0:T(2,128)} %pos_hbm.1, f32[2,1024]{1,0:T(2,128)} %dir_hbm.1, f32[1,1024]{1,0:T(1,128)} %bitcast.2, f32[1,1024]{1,0:T(1,128)} %bitcast.3, f32[3,64,64]{2,1,0:T(8,128)} %grad_hbm.1), custom_call_target="tpu_custom_call" | custom-call | tf_op jit(solution)/shard_map/ray_wave/pallas_call | solution.py:520
  35.4 0.6 %copy.9 = f32[3,64,64]{2,1,0:T(8,128)} copy(f32[3,64,64]{2,1,0:T(8,128)S(1)} %get-tuple-element.4) | data formatting | bytes 98304
  36.0 0.6 %copy.10 = f32[6,1024]{1,0:T(8,128)} copy(f32[6,1024]{1,0:T(8,128)S(1)} %get-tuple-element.5) | data formatting | bytes 49152
